TPU v7x, 32 devices: a whole 2x2x4 slice. The times are simulated.
32 devices in a mesh: wide: 8 (over y, x, core), narrow: 4 (over z).
Axes of the slice: x: 2, y: 2, z: 4, core: 2. Of those that a mesh axis runs over, the one named last changes fastest.
Arguments:
- vectors: bfloat16 [3, 4096, 128], P(None, ('wide', 'narrow')), may hold values from -18 to 18
- hessian: bfloat16 [3, 3, 61, 4096], P(None, None, None, ('wide', 'narrow')), may hold values from -0.9 to 5.4
- neighbours: int32 [60, 4096], P(None, ('wide', 'narrow')), may hold values from 0 to 415
- halo_atoms: int32 [1024], P(('wide', 'narrow')), may hold values from 0 to 127
- labels: int32 [4096], P(('wide', 'narrow')), may hold values from 0 to 15
- masses: float32 [2, 16], replicated, may hold values from 1 to 32
- rotation: float32 [2, 128, 128], replicated, may hold values from -0.5 to 0.5
Outputs:
- gram: float32 [2, 128, 128], replicated
- rotated: bfloat16 [2, 3, 4096, 128], P(None, None, ('wide', 'narrow'))
Inputs may be any that keep to these rules, and one draw needn't show every extreme that they name: `neighbours`: A row below 128 is a local atom of the domain; a row r at or above it is boundary atom (r - 128) % 32 of block (r - 128) // 32 in the 3x3 order of the steps.
All inputs are finite; a program needn't handle non-finite values.
Results may differ from a plain program's by a relative error of at most 0.003.
Values may be sent and summed in bfloat16 or wider, within the bound.
No kernel may reach another device: no remote copies, remote signals or barrier semaphores. Data moves between devices by JAX's collectives and lax.ppermute only.
A program may use at most 64 MiB of HBM per device.

v0:
```python
import jax
import jax.numpy as jnp
from jax import lax
from jax.sharding import PartitionSpec as P


def padded(array, sides, width):
    for axis, dim in sides:
        size, length = (lax.axis_size(axis), array.shape[dim])
        up = [(i, (i + 1) % size) for i in range(size - 1)]
        down = [(j, i) for i, j in up]
        last = lax.slice_in_dim(array, length - width, length, axis=dim)
        leading = lax.slice_in_dim(array, 0, width, axis=dim)
        before = lax.ppermute(last, axis, up)
        after = lax.ppermute(leading, axis, down)
        array = jnp.concatenate([before, array, after], axis=dim)
    return array


def class_factors(inverse_roots, classes):
    onehot = (
        classes[None, :] == jnp.arange(inverse_roots.shape[1], dtype=jnp.int32)[:, None]
    ).astype(jnp.float32)
    return jnp.dot(inverse_roots, onehot, precision=lax.Precision.HIGHEST)


def scale_rows(rows_full, factors):
    return jnp.concatenate(
        [rows_full * factors[0][None, :, None], rows_full * factors[1][None, :, None]], axis=2
    ).astype(jnp.bfloat16)


def local(vectors, hessian, neighbours, halo_atoms, labels, masses, rotation):
    atoms_here = vectors.shape[1]
    width = vectors.shape[2]
    boundary = halo_atoms.shape[0]
    inverse_roots = lax.rsqrt(masses)
    factors = class_factors(inverse_roots, labels)
    vector_complete = vectors.astype(jnp.float32)
    scaled = scale_rows(vector_complete, factors)
    outgoing = jnp.take(scaled, halo_atoms, axis=1)[:, None, None]
    rims = padded(outgoing, (("wide", 1), ("narrow", 2)), 1)
    rim_rows = rims.reshape(3, 9 * boundary, 2 * width)
    extended = jnp.concatenate([scaled, rim_rows], axis=1)
    total = jnp.einsum("ija,jac->iac", hessian[:, :, 0], scaled, preferred_element_type=jnp.float32)

    def add_group(group, running):
        blocks = lax.dynamic_slice_in_dim(hessian, 1 + group * 4, 4, 2)
        indices = lax.dynamic_slice_in_dim(neighbours, group * 4, 4, 0)
        picked = jnp.take(extended, indices.reshape(-1), axis=1).reshape(
            3, 4, atoms_here, 2 * width
        )
        return running + jnp.einsum(
            "ijka,jkac->iac", blocks, picked, preferred_element_type=jnp.float32
        )

    total = lax.fori_loop(0, neighbours.shape[0] // 4, add_group, total)
    hydrogen_image = total[:, :, :width] * factors[0][None, :, None]
    deuterium_image = total[:, :, width:] * factors[1][None, :, None]
    partial_gram = jnp.stack(
        [
            jnp.einsum(
                "eqv,eqh->vh", vector_complete, hydrogen_image, precision=lax.Precision.HIGHEST
            ),
            jnp.einsum(
                "eqv,eqh->vh", vector_complete, deuterium_image, precision=lax.Precision.HIGHEST
            ),
        ]
    )
    atoms_all = 3.0 * atoms_here * lax.axis_size("wide") * lax.axis_size("narrow")
    images = (hydrogen_image, deuterium_image)
    gram = lax.psum(partial_gram, ("wide", "narrow")) / atoms_all
    outputs = []
    for isotope_variant in range(2):
        fresh_block = images[isotope_variant] - jnp.einsum(
            "jyx,xs->jys", vector_complete, gram[isotope_variant], precision=lax.Precision.HIGHEST
        )
        outputs.append(
            jnp.einsum(
                "jyx,xs->jys",
                fresh_block,
                rotation[isotope_variant],
                precision=lax.Precision.HIGHEST,
            ).astype(jnp.bfloat16)
        )
    return (gram, jnp.stack(outputs))


def solution(mesh):
    return jax.shard_map(
        local,
        mesh=mesh,
        in_specs=(
            P(None, ("wide", "narrow"), None),
            P(None, None, None, ("wide", "narrow")),
            P(None, ("wide", "narrow")),
            P(("wide", "narrow")),
            P(("wide", "narrow")),
            P(),
            P(),
        ),
        out_specs=(P(), P(None, None, ("wide", "narrow"), None)),
        check_vma=False,
    )
```

profile of v0, /device:TPU:0, one launch (start us, length us, event | category | flops | bytes accessed | tf_op | source)
XLA Modules:
  0.0 256.6 jit_solution(16522191547537341307)
XLA Ops:
  8.5 0.8 convolution_bitcast_fusion.6
  9.4 1.0 fusion.8
  11.3 1.3 collective-permute-start.1
  12.6 3.0 %collective-permute-start = (bf16[3,1,1,32,256]{4,0,3,2,1:T(4,128)(2,1)S(1)}, bf16[3,1,1,32,256]{4,0,3,2,1:T(4,128)(2,1)S(1)}, u32[]{:S(2)}, u32[]{:S(2)}) collective-permute-start(bf16[3,1,1,32,256]{4,0,3,2,1:T(4,128)(2,1)S(1)} %bitcast_select_fusion), channel_id=1, source_target_pairs={{0,4},{4,8},{8,12},{12,16},{16,20},{20,24},{24,28},{1,5},{5,9},{9,... | collective-permute-start | bytes 147464 | tf_op jit(solution)/shard_map/ppermute | solution.py:14
  16.8 1.3 collective-permute-start.3
  18.1 5.6 %collective-permute-start.2 = (bf16[3,3,1,32,256]{4,0,3,2,1:T(4,128)(2,1)S(1)}, bf16[3,3,1,32,256]{4,0,3,2,1:T(4,128)(2,1)S(1)}, u32[]{:S(2)}, u32[]{:S(2)}) collective-permute-start(bf16[3,3,1,32,256]{4,0,3,2,1:T(4,128)(2,1)S(1)} %pad_maximum_fusion.3), channel_id=1, source_target_pairs={{0,1},{1,2},{2,3},{4,5},{5,6},{6,7},{8,9},{9,10},{10,11},{12,13},{... | collective-permute-start | bytes 442376 | tf_op jit(solution)/shard_map/ppermute | solution.py:14
  24.0 2.6 %collective-permute-done.3 = bf16[3,3,1,32,256]{4,0,3,2,1:T(4,128)(2,1)S(1)} collective-permute-done((bf16[3,3,1,32,256]{4,0,3,2,1:T(4,128)(2,1)S(1)}, bf16[3,3,1,32,256]{4,0,3,2,1:T(4,128)(2,1)S(1)}, u32[]{:S(2)}, u32[]{:S(2)}) %collective-permute-start.3) | collective-permute-done | bytes 147488 | tf_op jit(solution)/shard_map/ppermute | solution.py:15
  26.5 1.7 collective-permute-done.2
  29.5 86.3 %while.15 = (s32[]{:T(128)}, f32[3,128,256]{2,0,1:T(4,128)S(1)}, s32[60,128]{1,0:T(8,128)}, bf16[3,416,256]{2,0,1:T(4,128)(2,1)S(1)}, bf16[3,3,61,128]{3,2,1,0:T...) while((s32[]{:T(128)}, f32[3,128,256]{2,0,1:T(4,128)S(1)}, ...), condition=%wide.region_1.2_spmd, body=%wide.region_0.1_spmd.sunk | while | flops 2856458 | bytes 3210441 | solution.py:57
  30.3 0.8 constant_dynamic-slice_fusion.4
  31.5 2.4 gather_fusion
  33.9 1.4 fusion.30
  37.2 2.4 gather_fusion
  39.6 1.4 fusion.30
  41.8 0.8 constant_dynamic-slice_fusion.4
  43.0 2.4 gather_fusion
  45.4 1.4 fusion.30
  48.7 2.4 gather_fusion
  51.1 1.4 fusion.30
  53.3 0.8 constant_dynamic-slice_fusion.4
  54.5 2.4 gather_fusion
  56.9 1.4 fusion.30
  59.0 0.8 constant_dynamic-slice_fusion.4
  60.2 2.4 gather_fusion
  62.6 1.4 fusion.30
  66.0 2.4 gather_fusion
  68.4 1.4 fusion.30
  70.5 0.8 constant_dynamic-slice_fusion.4
  71.7 2.4 gather_fusion
  74.2 1.4 fusion.30
  77.5 2.4 gather_fusion
  79.9 1.4 fusion.30
  82.1 0.8 constant_dynamic-slice_fusion.4
  83.3 2.4 gather_fusion
  85.7 1.4 fusion.30
  89.0 2.4 gather_fusion
  91.4 1.4 fusion.30
  93.6 0.8 constant_dynamic-slice_fusion.4
  94.8 2.4 gather_fusion
  97.2 1.4 fusion.30
  100.5 2.4 gather_fusion
  102.9 1.4 fusion.30
  106.3 2.4 gather_fusion
  108.7 1.4 fusion.30
  112.0 2.4 gather_fusion
  114.4 1.4 fusion.30
  117.4 128.8 %all-reduce.2.cloned.1.call-done = f32[2,128,128]{1,2,0:T(8,128)} async-done(((f32[2,128,128]{1,2,0:T(8,128)}), f32[2,128,128]{1,2,0:T(8,128)}) %all-reduce.2.cloned.1.call-update) | async-done | bytes 131088 | tf_op jit(solution)/shard_map/psum | solution.py:72
  246.3 0.9 broadcast_multiply_fusion
  (117 shorter events, 32.0 us)
Async XLA Ops:
  7.2 239.1 %all-reduce.2.cloned.1.call-start = ((), (), s32[]{:S(2)}) async-start(), calls=%async_computation | async-start | bytes 262144 | tf_op jit(solution)/shard_map/psum | solution.py:72
  11.3 5.3 %collective-permute-start.1 = (bf16[3,1,1,32,256]{4,0,3,2,1:T(4,128)(2,1)S(1)}, bf16[3,1,1,32,256]{4,0,3,2,1:T(4,128)(2,1)S(1)}, u32[]{:S(2)}, u32[]{:S(2)}) collective-permute-start(bf16[3,1,1,32,256]{4,0,3,2,1:T(4,128)(2,1)S(1)} %bitcast_select_fusion), channel_id=1, source_target_pairs={{4,0},{8,4},{12,8},{16,12},{20,16},{24,20},{28,24},{5,1},{9,5},{13... | collective-permute-start | bytes 147464 | tf_op jit(solution)/shard_map/ppermute | solution.py:15
  12.6 4.0 %collective-permute-start = (bf16[3,1,1,32,256]{4,0,3,2,1:T(4,128)(2,1)S(1)}, bf16[3,1,1,32,256]{4,0,3,2,1:T(4,128)(2,1)S(1)}, u32[]{:S(2)}, u32[]{:S(2)}) collective-permute-start(bf16[3,1,1,32,256]{4,0,3,2,1:T(4,128)(2,1)S(1)} %bitcast_select_fusion), channel_id=1, source_target_pairs={{0,4},{4,8},{8,12},{12,16},{16,20},{20,24},{24,28},{1,5},{5,9},{9,... | collective-permute-start | bytes 147464 | tf_op jit(solution)/shard_map/ppermute | solution.py:14
  16.8 9.8 %collective-permute-start.3 = (bf16[3,3,1,32,256]{4,0,3,2,1:T(4,128)(2,1)S(1)}, bf16[3,3,1,32,256]{4,0,3,2,1:T(4,128)(2,1)S(1)}, u32[]{:S(2)}, u32[]{:S(2)}) collective-permute-start(bf16[3,3,1,32,256]{4,0,3,2,1:T(4,128)(2,1)S(1)} %pad_maximum_fusion.3), channel_id=1, source_target_pairs={{1,0},{2,1},{3,2},{5,4},{6,5},{7,6},{9,8},{10,9},{11,10},{13,12},{... | collective-permute-start | bytes 442376 | tf_op jit(solution)/shard_map/ppermute | solution.py:15
  18.1 10.2 %collective-permute-start.2 = (bf16[3,3,1,32,256]{4,0,3,2,1:T(4,128)(2,1)S(1)}, bf16[3,3,1,32,256]{4,0,3,2,1:T(4,128)(2,1)S(1)}, u32[]{:S(2)}, u32[]{:S(2)}) collective-permute-start(bf16[3,3,1,32,256]{4,0,3,2,1:T(4,128)(2,1)S(1)} %pad_maximum_fusion.3), channel_id=1, source_target_pairs={{0,1},{1,2},{2,3},{4,5},{5,6},{6,7},{8,9},{9,10},{10,11},{12,13},{... | collective-permute-start | bytes 442376 | tf_op jit(solution)/shard_map/ppermute | solution.py:14
  29.5 86.4 %copy-start = (bf16[3,128,128]{2,1,0:T(8,128)(2,1)S(1)}, bf16[3,128,128]{2,1,0:T(8,128)(2,1)}, u32[]{:S(2)}) copy-start(bf16[3,128,128]{2,1,0:T(8,128)(2,1)} %param.9) | copy-start | bytes 294916
  116.7 131.7 %copy-start.1 = (f32[2,128,128]{2,1,0:T(8,128)S(1)}, f32[2,128,128]{2,1,0:T(8,128)}, u32[]{:S(2)}) copy-start(f32[2,128,128]{2,1,0:T(8,128)} %param.15) | copy-start | bytes 393220
Sparse Core Ops, SparseCore 0:
  117.5 128.6 all-reduce.1
where the time goes:
time: 258 us; the launch traced here: 257 us
  waiting for transfers between devices  133 us (52%)
  local copies, waits for them, and re-layouts  56.9 us (22%)
  matrix products  24.1 us (9%)
  other arithmetic  16.2 us (6%)
  between operations  14.2 us (6%)
  starting transfers between devices  11.3 us (4%)
    psum x1, waiting for transfers between devices, local(): gram = lax.psum(partial_gram, ('wide', 'narrow')) / atoms_all  129 us
    gather x15, local copies, waits for them, and re-layouts, add_group(): jnp.take(extended, indices.reshape(-1), axis=1)  36 us
    dot_general x15, matrix products, add_group(): jnp.einsum('ijka,jkac->iac', blocks, picked, preferred_element_type=jnp.f...  21.1 us
    dynamic_slice x30, local copies, waits for them, and re-layouts, add_group(): blocks = lax.dynamic_slice_in_dim(hessian, 1 + group * 4, 4, 2)  15.7 us
    and x15, other arithmetic, add_group(): jnp.take(extended, indices.reshape(-1), axis=1)  10.6 us
    ppermute x2, starting transfers between devices, padded(): before = lax.ppermute(last, axis, up)  8.63 us
  transfers between devices with their start and end apart: 5, of which 3 were waited for; matrix products, arithmetic and copies ran while one was open for 0% of the time, Pallas kernels for 0%

commit v1 on v0

v1 whole, which is shorter than its diff:
```python
import jax
import jax.numpy as jnp
from jax import lax
from jax.experimental import pallas as pl
from jax.experimental.pallas import tpu as pltpu
from jax.sharding import PartitionSpec as P

AXES = ("wide", "narrow")
F32 = jnp.float32
BF16 = jnp.bfloat16
I32 = jnp.int32
VMEM = pl.BlockSpec(memory_space=pltpu.VMEM)


def iota(shape, dim):
    return lax.broadcasted_iota(I32, shape, dim)


def split(x):
    hi = x.astype(BF16)
    return hi, (x - hi.astype(F32)).astype(BF16)


def dot(a, b):
    return jnp.dot(a, b, preferred_element_type=F32)


def column(row):
    n = row.shape[1]
    return jnp.sum(jnp.where(iota((n, n), 0) == iota((n, n), 1), row, 0), axis=1, keepdims=True)


def factor_rows(labels_row, masses):
    classes = masses.shape[1]
    hit = labels_row == iota((classes, labels_row.shape[1]), 0)
    roots = lax.rsqrt(masses)
    return [
        jnp.sum(jnp.where(hit, column(roots[v : v + 1]), 0.0), axis=0, keepdims=True)
        for v in range(2)
    ]


def boundary_kernel(vectors_ref, halo_ref, labels_ref, masses_ref, out_ref):
    atoms = vectors_ref.shape[1]
    width = vectors_ref.shape[2]
    bound = halo_ref.shape[1]
    factors = factor_rows(labels_ref[...], masses_ref[...])
    picks = column(halo_ref[...]) == iota((bound, atoms), 1)
    onehot = picks.astype(F32).astype(BF16)
    cols = [jnp.sum(jnp.where(picks, f, 0.0), axis=1, keepdims=True) for f in factors]
    for j in range(3):
        rows = dot(onehot, vectors_ref[j])
        for v in range(2):
            out_ref[j, :, v * width : (v + 1) * width] = (rows * cols[v]).astype(BF16)


def build_kernel(
    vectors_ref, hessian_ref, near_ref, labels_ref, masses_ref,
    m_ref, scaled_ref, factor_ref, vt_ref,
    near_scr, ht_scr, onehot_scr,
    *, n_wide, n_narrow, bound, rows_pad,
):
    atoms = vectors_ref.shape[1]
    width = vectors_ref.shape[2]
    slots = hessian_ref.shape[2]
    kpad = near_scr.shape[0]
    group = 16
    p = lax.axis_index("wide")
    q = lax.axis_index("narrow")
    near = near_ref[...]
    rel = near - atoms
    block = jnp.zeros_like(rel)
    for b in range(1, 9):
        block = block + (rel >= b * bound).astype(I32)
    bi = (block >= 3).astype(I32) + (block >= 6).astype(I32)
    bj = block - 3 * bi
    wp, zp = p + bi - 1, q + bj - 1
    inside = (wp >= 0) & (wp < n_wide) & (zp >= 0) & (zp < n_narrow)
    even_w, even_z = lax.rem(p, 2) == 0, lax.rem(q, 2) == 0
    up_w, down_w = jnp.where(even_w, 1, 2), jnp.where(even_w, 2, 1)
    up_z, down_z = jnp.where(even_z, 1, 2), jnp.where(even_z, 2, 1)
    sw = jnp.where(bi == 1, 0, jnp.where(bi == 2, up_w, down_w))
    sz = jnp.where(bj == 1, 0, jnp.where(bj == 2, up_z, down_z))
    placed = atoms + (sw * 3 + sz) * bound + (rel - block * bound)
    near = jnp.where(rel < 0, near, jnp.where(inside, placed, -1))
    near_scr[kpad - 8 :, :] = jnp.full((8, atoms), -1, I32)
    near_scr[0:1, :] = iota((1, atoms), 1)
    near_scr[1:slots, :] = near
    for c in range(3):
        for j in range(3):
            h = hessian_ref[c, j].astype(F32)
            h = jnp.concatenate([h, jnp.zeros((kpad - slots, atoms), F32)], axis=0)
            h = jnp.concatenate([h] * (atoms // kpad), axis=0)
            ht_scr[c * 3 + j] = h.T.astype(BF16)
    own = iota((group, group * kpad), 0) == iota((group, group * kpad), 1) // kpad
    own = own.astype(F32).astype(BF16)
    per = group * kpad // atoms
    lanes = iota((kpad, rows_pad), 1)

    def body(g, carry):
        base = pl.multiple_of(g * group, group)
        turned = pltpu.roll(near_scr[...], lax.rem(atoms - base, atoms), 1)
        for a in range(group):
            hit = turned[:, a : a + 1] == lanes
            onehot_scr[a * kpad : (a + 1) * kpad, :] = hit.astype(F32).astype(BF16)
        blocks = []
        for cj in range(9):
            h = ht_scr[cj, pl.ds(base, group), :]
            blocks.append(jnp.concatenate([h] * per, axis=1) * own)
        res = dot(jnp.concatenate(blocks, axis=0), onehot_scr[...])
        hi, lo = split(res)
        for c in range(3):
            for j in range(3):
                cj = c * 3 + j
                for t, part in enumerate((hi, lo)):
                    at = pl.multiple_of((t * 3 + c) * atoms + base, group)
                    m_ref[j, pl.ds(at, group), :] = part[cj * group : (cj + 1) * group]
        return carry

    lax.fori_loop(0, atoms // group, body, 0)
    factors = factor_rows(labels_ref[...], masses_ref[...])
    for v in range(2):
        f = jnp.broadcast_to(column(factors[v]), (atoms, width))
        factor_ref[v] = f
        for j in range(3):
            scaled_ref[j, :, v * width : (v + 1) * width] = (
                vectors_ref[j].astype(F32) * f
            ).astype(BF16)
    for j in range(3):
        vt_ref[:, j * atoms : (j + 1) * atoms] = vectors_ref[j].astype(F32).T.astype(BF16)


def apply_kernel(
    m_ref, scaled_ref, factor_ref, vt_ref, own_ref, ez_ref, oz_ref, ew_ref, ow_ref,
    image_ref, mine_ref, other_ref, ext_scr,
):
    atoms = scaled_ref.shape[1]
    width = vt_ref.shape[0]
    bound = own_ref.shape[1]
    rows_pad = ext_scr.shape[1]
    for j in range(3):
        ext_scr[j, :atoms] = scaled_ref[j]
        for s, ref in enumerate((own_ref, ez_ref, oz_ref)):
            ext_scr[j, atoms + s * bound : atoms + (s + 1) * bound] = ref[j]
        for s, ref in enumerate((ew_ref, ow_ref)):
            for z in range(3):
                at = atoms + (3 * (s + 1) + z) * bound
                ext_scr[j, at : at + bound] = ref[z, j]
        used = atoms + 9 * bound
        ext_scr[j, used:] = jnp.zeros((rows_pad - used, 2 * width), BF16)
    total = dot(m_ref[0], ext_scr[0]) + dot(m_ref[1], ext_scr[1]) + dot(m_ref[2], ext_scr[2])
    total = total[: 3 * atoms] + total[3 * atoms :]
    even = lax.rem(lax.axis_index("wide"), 2) == 0
    grams = []
    for v in range(2):
        f = factor_ref[v]
        image = total[:, v * width : (v + 1) * width] * jnp.concatenate([f] * 3, axis=0)
        image_ref[v] = image
        hi, lo = split(image)
        grams.append(dot(vt_ref[...], hi) + dot(vt_ref[...], lo))
    mine_ref[...] = jnp.where(even, grams[0], grams[1])
    other_ref[...] = jnp.where(even, grams[1], grams[0])


def turn_kernel(image_ref, rotation_ref, out_ref):
    for v in range(2):
        hi, lo = split(image_ref[v])
        rhi, rlo = split(rotation_ref[v])
        out_ref[v] = dot(hi, rhi) + (dot(lo, rhi) + dot(hi, rlo))


def final_kernel(
    mine_ref, other_ref, turned_ref, vectors_ref, rotation_ref, gram_ref, out_ref, *, count
):
    atoms = vectors_ref.shape[1]
    even = lax.rem(lax.axis_index("wide"), 2) == 0
    mine, other = mine_ref[...] / count, other_ref[...] / count
    for v in range(2):
        gram = jnp.where(even, mine, other) if v == 0 else jnp.where(even, other, mine)
        gram_ref[v] = gram
        hi, lo = split(gram)
        rhi, rlo = split(rotation_ref[v])
        step = dot(hi, rhi) + (dot(lo, rhi) + dot(hi, rlo))
        shi, slo = split(step)
        for j in range(3):
            vec = vectors_ref[j]
            turned = turned_ref[v, j * atoms : (j + 1) * atoms]
            out_ref[v, j] = (turned - (dot(vec, shi) + dot(vec, slo))).astype(BF16)


def swap(array, n_wide, n_narrow, place):
    pairs = []
    for p in range(n_wide):
        for q in range(n_narrow):
            a, b = place(p, q)
            pairs.append((p * n_narrow + q, a * n_narrow + b))
    return lax.ppermute(array, AXES, pairs)


def odd_partner(i, n):
    k = i + 1 if i % 2 else i - 1
    return k if 0 <= k < n else None


def call(kernel, out, *args, scratch=(), cost=None):
    shapes = [jax.ShapeDtypeStruct(s, d) for s, d in out]
    flops, moved = cost or (1000, 1000)
    return pl.pallas_call(
        kernel,
        out_shape=shapes,
        in_specs=[VMEM] * len(args),
        out_specs=[VMEM] * len(shapes),
        scratch_shapes=list(scratch),
        compiler_params=pltpu.CompilerParams(vmem_limit_bytes=24 * 2**20),
        cost_estimate=pl.CostEstimate(flops=flops, bytes_accessed=moved, transcendentals=0),
    )(*args)


def local(vectors, hessian, neighbours, halo_atoms, labels, masses, rotation):
    n_wide = lax.axis_size("wide")
    n_narrow = lax.axis_size("narrow")
    atoms, width = vectors.shape[1:]
    bound = halo_atoms.shape[0]
    slots = hessian.shape[2]
    kpad = -(-slots // 64) * 64
    rows = atoms + 9 * bound
    rows_pad = -(-rows // 128) * 128

    def exchange(array, place):
        return swap(array, n_wide, n_narrow, place)

    def odd_z(p, q):
        k = odd_partner(q, n_narrow)
        return (p ^ 1, q) if k is None else (p, k)

    def odd_w(p, q):
        k = odd_partner(p, n_wide)
        return (p, q ^ 1) if k is None else (k, q)

    labels_row = labels.reshape(1, atoms)
    halo_row = halo_atoms.reshape(1, bound)
    (rim,) = call(
        boundary_kernel, [((3, bound, 2 * width), BF16)], vectors, halo_row, labels_row, masses
    )
    ez = exchange(rim, lambda p, q: (p, q ^ 1))
    oz = exchange(rim, odd_z)

    def build(*refs):
        build_kernel(*refs, n_wide=n_wide, n_narrow=n_narrow, bound=bound, rows_pad=rows_pad)

    m, scaled, factor, vt = call(
        build,
        [
            ((3, 6 * atoms, rows_pad), BF16),
            ((3, atoms, 2 * width), BF16),
            ((2, atoms, width), F32),
            ((width, 3 * atoms), BF16),
        ],
        vectors, hessian, neighbours, labels_row, masses,
        scratch=[
            pltpu.VMEM((kpad, atoms), I32),
            pltpu.VMEM((9, atoms, atoms), BF16),
            pltpu.VMEM((16 * kpad, rows_pad), BF16),
        ],
        cost=(2 * 9 * atoms * 16 * kpad * rows_pad, 8 * 2**20),
    )
    three = jnp.stack([rim, ez, oz])
    ew = exchange(three, lambda p, q: (p ^ 1, q))
    ow = exchange(three, odd_w)
    image, mine, other = call(
        apply_kernel,
        [((2, 3 * atoms, width), F32), ((width, width), F32), ((width, width), F32)],
        m, scaled, factor, vt, rim, ez, oz, ew, ow,
        scratch=[pltpu.VMEM((3, rows_pad, 2 * width), BF16)],
        cost=(2 * 18 * atoms * rows_pad * 2 * width, 4 * 2**20),
    )
    (turned,) = call(
        turn_kernel, [((2, 3 * atoms, width), F32)], image, rotation,
        cost=(2 * 18 * atoms * width * width, 2**20),
    )
    total = mine + exchange(other, lambda p, q: (p ^ 1, q))
    bits = [(1 << k, 0) for k in range(1, n_wide.bit_length() - 1)]
    bits += [(0, 1 << k) for k in range(n_narrow.bit_length() - 1)]
    for k in range(0, len(bits), 2):
        steps = list(bits[k : k + 2])
        if len(steps) == 2:
            steps.insert(0, (steps[0][0] ^ steps[1][0], steps[0][1] ^ steps[1][1]))
        parts = [exchange(total, lambda p, q, s=s: (p ^ s[0], q ^ s[1])) for s in steps]
        for part in parts:
            total = total + part
    other = exchange(total, lambda p, q: (p ^ 1, q))
    count = 3.0 * atoms * n_wide * n_narrow

    def final(*refs):
        final_kernel(*refs, count=count)

    gram, rotated = call(
        final,
        [((2, width, width), F32), ((2, 3, atoms, width), BF16)],
        total, other, turned, vectors, rotation,
    )
    return gram, rotated


def solution(mesh):
    for size in mesh.shape.values():
        assert size & (size - 1) == 0 and size > 1
    return jax.shard_map(
        local,
        mesh=mesh,
        in_specs=(
            P(None, AXES, None),
            P(None, None, None, AXES),
            P(None, AXES),
            P(AXES),
            P(AXES),
            P(),
            P(),
        ),
        out_specs=(P(), P(None, None, AXES, None)),
        check_vma=False,
    )
```

time: 258 us -> 41.4 us (0.16)
  waiting for transfers between devices: 133 us -> 11.7 us
  local copies, waits for them, and re-layouts: 56.9 us -> 5.88 us
  matrix products: 24.1 us -> 0 us
  other arithmetic: 16.2 us -> 0.06 us
  between operations: 14.2 us -> 0.74 us
  Pallas kernels: 0 us -> 7.3 us
  starting transfers between devices: 11.3 us -> 15.4 us
    psum x1 -> x0, waiting for transfers between devices: 129 us -> none  [local(): gram = lax.psum(partial_gram, ('wide', 'narrow')) / atoms_all]
    gather x16 -> x0, local copies, waits for them, and re-layouts: 36.6 us -> none  [the longest x15 36 us: add_group(): jnp.take(extended, indices.reshape(-1), axis=1)]
    dot_general x23 -> x0, matrix products: 24.1 us -> none  [the longest x15 21.1 us: add_group(): jnp.einsum('ijka,jkac->iac', blocks, picked, preferred_element_type=jnp.f...]
    dynamic_slice x30 -> x0, local copies, waits for them, and re-layouts: 15.7 us -> none  [add_group(): blocks = lax.dynamic_slice_in_dim(hessian, 1 + group * 4, 4, 2)]
    and x16 -> x0, other arithmetic: 11.2 us -> none  [the longest x15 10.6 us: add_group(): jnp.take(extended, indices.reshape(-1), axis=1)]
    ppermute x4 -> x12, waiting for transfers between devices: 4.31 us -> 11.7 us  [swap(): return lax.ppermute(array, AXES, pairs)]
    pallas_call x0 -> x5, Pallas kernels: none -> 7.3 us  [call(): pl.pallas_call(kernel, out_shape=shapes, in_specs=[VMEM] * len(args), out...]
    unnamed x6 -> x18, local copies, waits for them, and re-layouts: 0.95 us -> 5.88 us
  transfers between devices with their start and end apart: 5 -> 12, of which waited for: 3 -> 8; matrix products, arithmetic and copies ran while one was open for 0% -> 0% of each run, Pallas kernels for 0% -> 11%
where the time goes in v1:
time: 41.4 us; the launch traced here: 41.1 us
  starting transfers between devices  15.4 us (37%)
  waiting for transfers between devices  11.7 us (28%)
  Pallas kernels  7.3 us (18%)
  local copies, waits for them, and re-layouts  5.88 us (14%)
  between operations  0.74 us (2%)
    ppermute x12, starting transfers between devices, swap(): return lax.ppermute(array, AXES, pairs)  15.4 us
    ppermute x12, waiting for transfers between devices, swap(): return lax.ppermute(array, AXES, pairs)  11.7 us
    pallas_call x5, Pallas kernels, call(): pl.pallas_call(kernel, out_shape=shapes, in_specs=[VMEM] * len(args), out...  7.3 us
    unnamed x18, local copies, waits for them, and re-layouts  5.88 us
  transfers between devices with their start and end apart: 12, of which 8 were waited for; matrix products, arithmetic and copies ran while one was open for 0% of the time, Pallas kernels for 11%

profile of v1, /device:TPU:0, one launch (start us, length us, event | category | flops | bytes accessed | tf_op | source)
XLA Modules:
  0.0 41.1 jit_solution(6501079646442657194)
XLA Ops:
  0.6 0.0 copy-start.1
  0.6 0.9 %copy-done.1 = bf16[3,128,128]{2,1,0:T(8,128)(2,1)S(1)} copy-done((bf16[3,128,128]{2,1,0:T(8,128)(2,1)S(1)}, bf16[3,128,128]{2,1,0:T(8,128)(2,1)}, u32[]{:S(2)}) %copy-start.1) | copy-done | bytes 98328
  1.5 0.0 copy-start.2
  1.5 0.7 %copy-done.2 = f32[2,16]{1,0:T(2,128)S(1)} copy-done((f32[2,16]{1,0:T(2,128)S(1)}, f32[2,16]{1,0:T(2,128)}, u32[]{:S(2)}) %copy-start.2) | copy-done | bytes 152
  2.2 0.0 copy-start.4
  2.2 0.7 %copy-done.4 = s32[32]{0:T(128)S(1)} copy-done((s32[32]{0:T(128)S(1)}, s32[32]{0:T(128)}, u32[]{:S(2)}) %copy-start.4) | copy-done | bytes 152
  2.9 0.0 copy-start.5
  2.9 0.7 %copy-done.5 = s32[128]{0:T(128)S(1)} copy-done((s32[128]{0:T(128)S(1)}, s32[128]{0:T(128)}, u32[]{:S(2)}) %copy-start.5) | copy-done | bytes 536
  3.5 0.2 shard_map.87.own_ref
  3.7 0.6 %collective-permute-start.1 = (bf16[3,32,256]{2,1,0:T(8,128)(2,1)S(1)}, bf16[3,32,256]{2,1,0:T(8,128)(2,1)S(1)}, u32[]{:S(2)}, u32[]{:S(2)}) collective-permute-start(bf16[3,32,256]{2,1,0:T(8,128)(2,1)S(1)} %shard_map.87.own_ref), channel_id=1, source_target_pairs={{0,4},{1,2},{2,1},{3,7},{4,0},{5,6},{6,5},{7,3},{8,12},{9,10},{10,... | collective-permute-start | bytes 147464 | tf_op jit(solution)/shard_map/ppermute | solution.py:197
  4.3 4.1 %collective-permute-start = (bf16[3,32,256]{2,1,0:T(8,128)(2,1)S(1)}, bf16[3,32,256]{2,1,0:T(8,128)(2,1)S(1)}, u32[]{:S(2)}, u32[]{:S(2)}) collective-permute-start(bf16[3,32,256]{2,1,0:T(8,128)(2,1)S(1)} %shard_map.87.own_ref), channel_id=1, source_target_pairs={{0,1},{1,0},{2,3},{3,2},{4,5},{5,4},{6,7},{7,6},{8,9},{9,8},{10,11... | collective-permute-start | bytes 147464 | tf_op jit(solution)/shard_map/ppermute | solution.py:197
  8.4 0.0 collective-permute-done.1.oz_ref
  8.4 2.1 %collective-permute-done.ez_ref = bf16[3,32,256]{2,1,0:T(8,128)(2,1)S(1)} collective-permute-done((bf16[3,32,256]{2,1,0:T(8,128)(2,1)S(1)}, bf16[3,32,256]{2,1,0:T(8,128)(2,1)S(1)}, u32[]{:S(2)}, u32[]{:S(2)}) %collective-permute-start) | collective-permute-done | bytes 49184 | tf_op jit(solution)/shard_map/ppermute | solution.py:197
  10.5 2.1 %collective-permute-start.3 = (bf16[3,3,32,256]{3,2,1,0:T(8,128)(2,1)S(1)}, bf16[3,3,32,256]{3,2,1,0:T(8,128)(2,1)S(1)}, u32[]{:S(2)}, u32[]{:S(2)}) collective-permute-start(bf16[3,3,32,256]{3,2,1,0:T(8,128)(2,1)S(1)} %pad_maximum_fusion), channel_id=1, source_target_pairs={{0,1},{1,0},{2,3},{3,2},{4,8},{5,9},{6,10},{7,11},{8,4},{9,5},{10,... | collective-permute-start | bytes 442376 | tf_op jit(solution)/shard_map/ppermute | solution.py:197
  12.6 0.0 collective-permute-start.2
  12.6 0.0 copy-start.3
  12.6 0.7 %copy-done.3 = f32[2,16]{1,0:T(2,128)S(1)} copy-done((f32[2,16]{1,0:T(2,128)S(1)}, f32[2,16]{1,0:T(2,128)}, u32[]{:S(2)}) %copy-start.3) | copy-done | bytes 152
  13.3 0.0 copy-start.6
  13.3 0.7 %copy-done.6 = s32[128]{0:T(128)S(1)} copy-done((s32[128]{0:T(128)S(1)}, s32[128]{0:T(128)}, u32[]{:S(2)}) %copy-start.6) | copy-done | bytes 536
  13.9 0.0 copy-start.7
  13.9 0.9 %copy-done.7 = bf16[3,3,61,128]{3,2,1,0:T(8,128)(2,1)S(1)} copy-done((bf16[3,3,61,128]{3,2,1,0:T(8,128)(2,1)S(1)}, bf16[3,3,61,128]{3,2,1,0:T(8,128)(2,1)}, u32[]{:S(2)}) %copy-start.7) | copy-done | bytes 140568
  14.9 0.0 copy-start.8
  14.9 0.8 %copy-done.8 = s32[60,128]{1,0:T(8,128)S(1)} copy-done((s32[60,128]{1,0:T(8,128)S(1)}, s32[60,128]{1,0:T(8,128)}, u32[]{:S(2)}) %copy-start.8) | copy-done | bytes 30744
  15.6 4.3 %shard_map.86 = (bf16[3,768,512]{2,1,0:T(8,128)(2,1)S(1)}, bf16[3,128,256]{2,1,0:T(8,128)(2,1)S(1)}, f32[2,128,128]{2,1,0:T(8,128)S(1)}, bf16[128,384]{1,0:T(8,128)(2,1)S(1)}) custom-call(bf16[3,128,128]{2,1,0:T(8,128)(2,1)S(1)} %copy-done.1, bf16[3,3,61,128]{3,2,1,0:T(8,128)(2,1)S(1)} %copy-done.7, s32[60,128]{1,0:T(8,128)S(1)} %copy-done.8, ...), custom_call_target="tpu_custom_call" | custom-call | flops 1207959552 | bytes 8388608 | tf_op jit(solution)/shard_map/pallas_call | solution.py:208
  19.9 0.0 copy-start
  19.9 0.0 collective-permute-done.3.ow_ref
  19.9 0.0 collective-permute-done.2.ew_ref
  19.9 1.2 %shard_map.88 = (f32[2,384,128]{2,1,0:T(8,128)S(1)}, f32[128,128]{1,0:T(8,128)S(1)}, f32[128,128]{1,0:T(8,128)S(1)}) custom-call(bf16[3,768,512]{2,1,0:T(8,128)(2,1)S(1)} %get-tuple-element.9.m_ref, bf16[3,128,256]{2,1,0:T(8,128)(2,1)S(1)} %get-tuple-element.10.scaled_ref, f32[2,128,128]{2,1,0:T(8,128)S(1)} %get-tuple-element.11.factor_ref, ...), custom_call_target="tpu_custom_call" | custom-call | flops 603979776 | bytes 4194304 | tf_op jit(solution)/shard_map/pallas_call | solution.py:208
  21.1 0.6 %collective-permute-start.4 = (f32[128,128]{1,0:T(8,128)S(1)}, f32[128,128]{1,0:T(8,128)S(1)}, u32[]{:S(2)}, u32[]{:S(2)}) collective-permute-start(f32[128,128]{1,0:T(8,128)S(1)} %get-tuple-element.14), channel_id=1, source_target_pairs={{0,4},{1,5},{2,6},{3,7},{4,0},{5,1},{6,2},{7,3},{8,12},{9,13},{10,... | collective-permute-start | bytes 196616 | tf_op jit(solution)/shard_map/ppermute | solution.py:197
  21.7 0.9 %collective-permute-done.4 = f32[128,128]{1,0:T(8,128)S(1)} collective-permute-done((f32[128,128]{1,0:T(8,128)S(1)}, f32[128,128]{1,0:T(8,128)S(1)}, u32[]{:S(2)}, u32[]{:S(2)}) %collective-permute-start.4) | collective-permute-done | bytes 65568 | tf_op jit(solution)/shard_map/ppermute | solution.py:197
  22.6 1.0 %collective-permute-start.7 = (f32[128,128]{1,0:T(8,128)S(1)}, f32[128,128]{1,0:T(8,128)S(1)}, u32[]{:S(2)}, u32[]{:S(2)}) collective-permute-start(f32[128,128]{1,0:T(8,128)S(1)} %add.21), channel_id=1, source_target_pairs={{0,16},{1,17},{2,18},{3,19},{4,20},{5,21},{6,22},{7,23},{8,24},{9,... | collective-permute-start | bytes 196616 | tf_op jit(solution)/shard_map/ppermute | solution.py:197
  23.6 0.2 collective-permute-start.6
  23.8 2.4 %collective-permute-start.5 = (f32[128,128]{1,0:T(8,128)S(1)}, f32[128,128]{1,0:T(8,128)S(1)}, u32[]{:S(2)}, u32[]{:S(2)}) collective-permute-start(f32[128,128]{1,0:T(8,128)S(1)} %add.21), channel_id=1, source_target_pairs={{0,24},{1,25},{2,26},{3,27},{4,28},{5,29},{6,30},{7,31},{8,16},{9,... | collective-permute-start | bytes 196616 | tf_op jit(solution)/shard_map/ppermute | solution.py:197
  26.2 0.9 %collective-permute-done.7 = f32[128,128]{1,0:T(8,128)S(1)} collective-permute-done((f32[128,128]{1,0:T(8,128)S(1)}, f32[128,128]{1,0:T(8,128)S(1)}, u32[]{:S(2)}, u32[]{:S(2)}) %collective-permute-start.7) | collective-permute-done | bytes 65568 | tf_op jit(solution)/shard_map/ppermute | solution.py:197
  27.0 1.5 %collective-permute-done.6 = f32[128,128]{1,0:T(8,128)S(1)} collective-permute-done((f32[128,128]{1,0:T(8,128)S(1)}, f32[128,128]{1,0:T(8,128)S(1)}, u32[]{:S(2)}, u32[]{:S(2)}) %collective-permute-start.6) | collective-permute-done | bytes 65568 | tf_op jit(solution)/shard_map/ppermute | solution.py:197
  28.5 1.1 %collective-permute-done.5 = f32[128,128]{1,0:T(8,128)S(1)} collective-permute-done((f32[128,128]{1,0:T(8,128)S(1)}, f32[128,128]{1,0:T(8,128)S(1)}, u32[]{:S(2)}, u32[]{:S(2)}) %collective-permute-start.5) | collective-permute-done | bytes 65568 | tf_op jit(solution)/shard_map/ppermute | solution.py:197
  29.6 1.5 %collective-permute-start.10 = (f32[128,128]{1,0:T(8,128)S(1)}, f32[128,128]{1,0:T(8,128)S(1)}, u32[]{:S(2)}, u32[]{:S(2)}) collective-permute-start(f32[128,128]{1,0:T(8,128)S(1)} %add_add_fusion.1), channel_id=1, source_target_pairs={{0,2},{1,3},{2,0},{3,1},{4,6},{5,7},{6,4},{7,5},{8,10},{9,11},{10,... | collective-permute-start | bytes 196616 | tf_op jit(solution)/shard_map/ppermute | solution.py:197
  31.2 1.2 %collective-permute-start.9 = (f32[128,128]{1,0:T(8,128)S(1)}, f32[128,128]{1,0:T(8,128)S(1)}, u32[]{:S(2)}, u32[]{:S(2)}) collective-permute-start(f32[128,128]{1,0:T(8,128)S(1)} %add_add_fusion.1), channel_id=1, source_target_pairs={{0,1},{1,0},{2,3},{3,2},{4,5},{5,4},{6,7},{7,6},{8,9},{9,8},{10,11... | collective-permute-start | bytes 196616 | tf_op jit(solution)/shard_map/ppermute | solution.py:197
  32.4 1.7 %collective-permute-start.8 = (f32[128,128]{1,0:T(8,128)S(1)}, f32[128,128]{1,0:T(8,128)S(1)}, u32[]{:S(2)}, u32[]{:S(2)}) collective-permute-start(f32[128,128]{1,0:T(8,128)S(1)} %add_add_fusion.1), channel_id=1, source_target_pairs={{0,3},{1,2},{2,1},{3,0},{4,7},{5,6},{6,5},{7,4},{8,11},{9,10},{10,... | collective-permute-start | bytes 196616 | tf_op jit(solution)/shard_map/ppermute | solution.py:197
  34.1 2.6 %collective-permute-done.10 = f32[128,128]{1,0:T(8,128)S(1)} collective-permute-done((f32[128,128]{1,0:T(8,128)S(1)}, f32[128,128]{1,0:T(8,128)S(1)}, u32[]{:S(2)}, u32[]{:S(2)}) %collective-permute-start.10) | collective-permute-done | bytes 65568 | tf_op jit(solution)/shard_map/ppermute | solution.py:197
  36.7 0.0 collective-permute-done.9
  36.7 1.7 %collective-permute-done.8 = f32[128,128]{1,0:T(8,128)S(1)} collective-permute-done((f32[128,128]{1,0:T(8,128)S(1)}, f32[128,128]{1,0:T(8,128)S(1)}, u32[]{:S(2)}, u32[]{:S(2)}) %collective-permute-start.8) | collective-permute-done | bytes 65568 | tf_op jit(solution)/shard_map/ppermute | solution.py:197
  38.4 0.1 collective-permute-start.11
  38.5 0.0 copy-done
  38.5 0.3 shard_map.89.refs_2_
  38.8 0.9 %collective-permute-done.11.refs_1_ = f32[128,128]{1,0:T(8,128)S(1)} collective-permute-done((f32[128,128]{1,0:T(8,128)S(1)}, f32[128,128]{1,0:T(8,128)S(1)}, u32[]{:S(2)}, u32[]{:S(2)}) %collective-permute-start.11) | collective-permute-done | bytes 65568 | tf_op jit(solution)/shard_map/ppermute | solution.py:197
  39.8 1.3 %shard_map.90 = (f32[2,128,128]{2,1,0:T(8,128)}, bf16[2,3,128,128]{3,2,1,0:T(8,128)(2,1)}) custom-call(f32[128,128]{1,0:T(8,128)S(1)} %add_add_fusion.refs_0_, f32[128,128]{1,0:T(8,128)S(1)} %collective-permute-done.11.refs_1_, f32[2,384,128]{2,1,0:T(8,128)S(1)} %shard_map.89.refs_2_, bf16[3,128,128]{2,1,0:T(8,128)(2,1)S(1)} %copy-done.1, ...), custom_call_target="tpu_custom_call" | custom-call | flops 1000 | bytes 1000 | tf_op jit(solution)/shard_map/pallas_call | solution.py:208
  (4 shorter events, 0.1 us)
Async XLA Ops:
  0.6 0.9 %copy-start.1 = (bf16[3,128,128]{2,1,0:T(8,128)(2,1)S(1)}, bf16[3,128,128]{2,1,0:T(8,128)(2,1)}, u32[]{:S(2)}) copy-start(bf16[3,128,128]{2,1,0:T(8,128)(2,1)} %refs_3_.1) | copy-start | bytes 294916
  1.5 0.7 %copy-start.2 = (f32[2,16]{1,0:T(2,128)S(1)}, f32[2,16]{1,0:T(2,128)}, u32[]{:S(2)}) copy-start(f32[2,16]{1,0:T(2,128)} %masses_ref.1) | copy-start | bytes 388
  2.2 0.7 %copy-start.4 = (s32[32]{0:T(128)S(1)}, s32[32]{0:T(128)}, u32[]{:S(2)}) copy-start(s32[32]{0:T(128)} %param.10) | copy-start | bytes 388
  2.9 0.7 %copy-start.5 = (s32[128]{0:T(128)S(1)}, s32[128]{0:T(128)}, u32[]{:S(2)}) copy-start(s32[128]{0:T(128)} %param.11) | copy-start | bytes 1540
  3.7 4.7 %collective-permute-start.1 = (bf16[3,32,256]{2,1,0:T(8,128)(2,1)S(1)}, bf16[3,32,256]{2,1,0:T(8,128)(2,1)S(1)}, u32[]{:S(2)}, u32[]{:S(2)}) collective-permute-start(bf16[3,32,256]{2,1,0:T(8,128)(2,1)S(1)} %shard_map.87.own_ref), channel_id=1, source_target_pairs={{0,4},{1,2},{2,1},{3,7},{4,0},{5,6},{6,5},{7,3},{8,12},{9,10},{10,... | collective-permute-start | bytes 147464 | tf_op jit(solution)/shard_map/ppermute | solution.py:197
  4.3 6.2 %collective-permute-start = (bf16[3,32,256]{2,1,0:T(8,128)(2,1)S(1)}, bf16[3,32,256]{2,1,0:T(8,128)(2,1)S(1)}, u32[]{:S(2)}, u32[]{:S(2)}) collective-permute-start(bf16[3,32,256]{2,1,0:T(8,128)(2,1)S(1)} %shard_map.87.own_ref), channel_id=1, source_target_pairs={{0,1},{1,0},{2,3},{3,2},{4,5},{5,4},{6,7},{7,6},{8,9},{9,8},{10,11... | collective-permute-start | bytes 147464 | tf_op jit(solution)/shard_map/ppermute | solution.py:197
  10.5 9.4 %collective-permute-start.3 = (bf16[3,3,32,256]{3,2,1,0:T(8,128)(2,1)S(1)}, bf16[3,3,32,256]{3,2,1,0:T(8,128)(2,1)S(1)}, u32[]{:S(2)}, u32[]{:S(2)}) collective-permute-start(bf16[3,3,32,256]{3,2,1,0:T(8,128)(2,1)S(1)} %pad_maximum_fusion), channel_id=1, source_target_pairs={{0,1},{1,0},{2,3},{3,2},{4,8},{5,9},{6,10},{7,11},{8,4},{9,5},{10,... | collective-permute-start | bytes 442376 | tf_op jit(solution)/shard_map/ppermute | solution.py:197
  12.6 7.3 %collective-permute-start.2 = (bf16[3,3,32,256]{3,2,1,0:T(8,128)(2,1)S(1)}, bf16[3,3,32,256]{3,2,1,0:T(8,128)(2,1)S(1)}, u32[]{:S(2)}, u32[]{:S(2)}) collective-permute-start(bf16[3,3,32,256]{3,2,1,0:T(8,128)(2,1)S(1)} %pad_maximum_fusion), channel_id=1, source_target_pairs={{0,4},{1,5},{2,6},{3,7},{4,0},{5,1},{6,2},{7,3},{8,12},{9,13},{10,... | collective-permute-start | bytes 442376 | tf_op jit(solution)/shard_map/ppermute | solution.py:197
  12.6 0.7 %copy-start.3 = (f32[2,16]{1,0:T(2,128)S(1)}, f32[2,16]{1,0:T(2,128)}, u32[]{:S(2)}) copy-start(f32[2,16]{1,0:T(2,128)} %masses_ref.1) | copy-start | bytes 388
  13.3 0.7 %copy-start.6 = (s32[128]{0:T(128)S(1)}, s32[128]{0:T(128)}, u32[]{:S(2)}) copy-start(s32[128]{0:T(128)} %param.11) | copy-start | bytes 1540
  13.9 0.9 %copy-start.7 = (bf16[3,3,61,128]{3,2,1,0:T(8,128)(2,1)S(1)}, bf16[3,3,61,128]{3,2,1,0:T(8,128)(2,1)}, u32[]{:S(2)}) copy-start(bf16[3,3,61,128]{3,2,1,0:T(8,128)(2,1)} %refs_1_.1) | copy-start | bytes 421636
  14.9 0.8 %copy-start.8 = (s32[60,128]{1,0:T(8,128)S(1)}, s32[60,128]{1,0:T(8,128)}, u32[]{:S(2)}) copy-start(s32[60,128]{1,0:T(8,128)} %refs_2_.1) | copy-start | bytes 92164
  19.9 18.6 %copy-start = (f32[2,128,128]{2,1,0:T(8,128)S(1)}, f32[2,128,128]{2,1,0:T(8,128)}, u32[]{:S(2)}) copy-start(f32[2,128,128]{2,1,0:T(8,128)} %refs_4_.3) | copy-start | bytes 393220
  21.1 1.5 %collective-permute-start.4 = (f32[128,128]{1,0:T(8,128)S(1)}, f32[128,128]{1,0:T(8,128)S(1)}, u32[]{:S(2)}, u32[]{:S(2)}) collective-permute-start(f32[128,128]{1,0:T(8,128)S(1)} %get-tuple-element.14), channel_id=1, source_target_pairs={{0,4},{1,5},{2,6},{3,7},{4,0},{5,1},{6,2},{7,3},{8,12},{9,13},{10,... | collective-permute-start | bytes 196616 | tf_op jit(solution)/shard_map/ppermute | solution.py:197
  22.6 4.4 %collective-permute-start.7 = (f32[128,128]{1,0:T(8,128)S(1)}, f32[128,128]{1,0:T(8,128)S(1)}, u32[]{:S(2)}, u32[]{:S(2)}) collective-permute-start(f32[128,128]{1,0:T(8,128)S(1)} %add.21), channel_id=1, source_target_pairs={{0,16},{1,17},{2,18},{3,19},{4,20},{5,21},{6,22},{7,23},{8,24},{9,... | collective-permute-start | bytes 196616 | tf_op jit(solution)/shard_map/ppermute | solution.py:197
  23.6 4.9 %collective-permute-start.6 = (f32[128,128]{1,0:T(8,128)S(1)}, f32[128,128]{1,0:T(8,128)S(1)}, u32[]{:S(2)}, u32[]{:S(2)}) collective-permute-start(f32[128,128]{1,0:T(8,128)S(1)} %add.21), channel_id=1, source_target_pairs={{0,8},{1,9},{2,10},{3,11},{4,12},{5,13},{6,14},{7,15},{8,0},{9,1},... | collective-permute-start | bytes 196616 | tf_op jit(solution)/shard_map/ppermute | solution.py:197
  23.8 5.8 %collective-permute-start.5 = (f32[128,128]{1,0:T(8,128)S(1)}, f32[128,128]{1,0:T(8,128)S(1)}, u32[]{:S(2)}, u32[]{:S(2)}) collective-permute-start(f32[128,128]{1,0:T(8,128)S(1)} %add.21), channel_id=1, source_target_pairs={{0,24},{1,25},{2,26},{3,27},{4,28},{5,29},{6,30},{7,31},{8,16},{9,... | collective-permute-start | bytes 196616 | tf_op jit(solution)/shard_map/ppermute | solution.py:197
  29.6 7.1 %collective-permute-start.10 = (f32[128,128]{1,0:T(8,128)S(1)}, f32[128,128]{1,0:T(8,128)S(1)}, u32[]{:S(2)}, u32[]{:S(2)}) collective-permute-start(f32[128,128]{1,0:T(8,128)S(1)} %add_add_fusion.1), channel_id=1, source_target_pairs={{0,2},{1,3},{2,0},{3,1},{4,6},{5,7},{6,4},{7,5},{8,10},{9,11},{10,... | collective-permute-start | bytes 196616 | tf_op jit(solution)/shard_map/ppermute | solution.py:197
  31.2 5.6 %collective-permute-start.9 = (f32[128,128]{1,0:T(8,128)S(1)}, f32[128,128]{1,0:T(8,128)S(1)}, u32[]{:S(2)}, u32[]{:S(2)}) collective-permute-start(f32[128,128]{1,0:T(8,128)S(1)} %add_add_fusion.1), channel_id=1, source_target_pairs={{0,1},{1,0},{2,3},{3,2},{4,5},{5,4},{6,7},{7,6},{8,9},{9,8},{10,11... | collective-permute-start | bytes 196616 | tf_op jit(solution)/shard_map/ppermute | solution.py:197
  32.4 6.1 %collective-permute-start.8 = (f32[128,128]{1,0:T(8,128)S(1)}, f32[128,128]{1,0:T(8,128)S(1)}, u32[]{:S(2)}, u32[]{:S(2)}) collective-permute-start(f32[128,128]{1,0:T(8,128)S(1)} %add_add_fusion.1), channel_id=1, source_target_pairs={{0,3},{1,2},{2,1},{3,0},{4,7},{5,6},{6,5},{7,4},{8,11},{9,10},{10,... | collective-permute-start | bytes 196616 | tf_op jit(solution)/shard_map/ppermute | solution.py:197
  38.4 1.3 %collective-permute-start.11 = (f32[128,128]{1,0:T(8,128)S(1)}, f32[128,128]{1,0:T(8,128)S(1)}, u32[]{:S(2)}, u32[]{:S(2)}) collective-permute-start(f32[128,128]{1,0:T(8,128)S(1)} %add_add_fusion.refs_0_), channel_id=1, source_target_pairs={{0,4},{1,5},{2,6},{3,7},{4,0},{5,1},{6,2},{7,3},{8,12},{9,13},{10,... | collective-permute-start | bytes 196616 | tf_op jit(solution)/shard_map/ppermute | solution.py:197

commit v2 on v1

v2 whole, which is shorter than its diff:
```python
import jax
import jax.numpy as jnp
from jax import lax
from jax.experimental import pallas as pl
from jax.experimental.pallas import tpu as pltpu
from jax.sharding import PartitionSpec as P

AXES = ("wide", "narrow")
F32 = jnp.float32
BF16 = jnp.bfloat16
I32 = jnp.int32
VMEM = pl.BlockSpec(memory_space=pltpu.VMEM)


def iota(shape, dim):
    return lax.broadcasted_iota(I32, shape, dim)


def split(x):
    hi = x.astype(BF16)
    return hi, (x - hi.astype(F32)).astype(BF16)


def dot(a, b):
    return jnp.dot(a, b, preferred_element_type=F32)


def column(row):
    n = row.shape[1]
    return jnp.sum(jnp.where(iota((n, n), 0) == iota((n, n), 1), row, 0), axis=1, keepdims=True)


def factor_rows(labels_row, masses):
    classes = masses.shape[1]
    hit = labels_row == iota((classes, labels_row.shape[1]), 0)
    roots = lax.rsqrt(masses)
    return [
        jnp.sum(jnp.where(hit, column(roots[v : v + 1]), 0.0), axis=0, keepdims=True)
        for v in range(2)
    ]


def prepare_kernel(
    vectors_hbm, halo_hbm, labels_hbm, masses_hbm, near_hbm, hessian_hbm, rotation_hbm,
    rim_ref, vectors_ref, labels_ref, masses_ref, near_ref, hessian_ref, rotation_ref,
    halo_ref, sems,
):
    pairs = (
        (vectors_hbm, vectors_ref), (halo_hbm, halo_ref), (labels_hbm, labels_ref),
        (masses_hbm, masses_ref), (near_hbm, near_ref), (hessian_hbm, hessian_ref),
        (rotation_hbm, rotation_ref),
    )
    copies = [pltpu.make_async_copy(a, b, sems.at[i]) for i, (a, b) in enumerate(pairs)]
    for copy in copies:
        copy.start()
    for copy in copies[:4]:
        copy.wait()
    atoms, width = vectors_ref.shape[1:]
    bound = halo_ref.shape[1]
    factors = factor_rows(labels_ref[...], masses_ref[...])
    picks = column(halo_ref[...]) == iota((bound, atoms), 1)
    onehot = picks.astype(F32).astype(BF16)
    for j in range(3):
        rim_ref[j] = dot(onehot, vectors_ref[j]).astype(BF16)
    lane = iota((bound, width), 1)
    packed = jnp.zeros((bound, width), F32)
    for v in range(2):
        rest = jnp.sum(jnp.where(picks, factors[v], 0.0), axis=1, keepdims=True)
        for k in range(3):
            part = rest.astype(BF16).astype(F32)
            packed = jnp.where(lane == 3 * v + k, part, packed)
            rest = rest - part
    rim_ref[3] = packed.astype(BF16)
    for copy in copies[4:]:
        copy.wait()


def scale_rows(blocks, ext_ref, base):
    bound, width = blocks[0].shape[1:]
    count = bound * len(blocks)
    shape = (width, 2 * width)
    spread = (iota(shape, 0) // 3 == iota(shape, 1) // width).astype(F32).astype(BF16)
    factor = dot(jnp.concatenate([b[3] for b in blocks], axis=0), spread)
    for j in range(3):
        rows = jnp.concatenate([b[j] for b in blocks], axis=0).astype(F32)
        rows = jnp.concatenate([rows, rows], axis=1) * factor
        ext_ref[j, base : base + count] = rows.astype(BF16)


def one_group(near, ht_ref, onehot_scr, store, g, group):
    kpad, atoms = near.shape
    lanes = iota((kpad, onehot_scr.shape[1]), 1)
    shape = (group, group * kpad)
    own = (iota(shape, 0) == iota(shape, 1) // kpad).astype(F32).astype(BF16)
    per = group * kpad // atoms
    for a in range(group):
        at = g * group + a
        hit = near[:, at : at + 1] == lanes
        onehot_scr[a * kpad : (a + 1) * kpad, :] = hit.astype(F32).astype(BF16)
    blocks = []
    for cj in range(9):
        h = ht_ref[cj, g * group : (g + 1) * group, :]
        blocks.append(jnp.concatenate([h] * per, axis=1) * own)
    res = dot(jnp.concatenate(blocks, axis=0), onehot_scr[...])
    for cj in range(9):
        hi, lo = split(res[cj * group : (cj + 1) * group])
        store(cj // 3, cj % 3, hi, lo)


def first_kernel(
    near_in, hessian_ref, m_ref, near_ref, ht_ref, onehot_scr, *, n_wide, n_narrow, bound, w_base
):
    atoms = near_in.shape[1]
    slots = hessian_ref.shape[2]
    kpad = near_ref.shape[0]
    group = 16
    p = lax.axis_index("wide")
    q = lax.axis_index("narrow")
    near = near_in[...]
    rel = near - atoms
    block = jnp.zeros_like(rel)
    for b in range(1, 9):
        block = block + (rel >= b * bound).astype(I32)
    bi = (block >= 3).astype(I32) + (block >= 6).astype(I32)
    bj = block - 3 * bi
    wp, zp = p + bi - 1, q + bj - 1
    inside = (wp >= 0) & (wp < n_wide) & (zp >= 0) & (zp < n_narrow)
    even_w, even_z = lax.rem(p, 2) == 0, lax.rem(q, 2) == 0
    up_w, down_w = jnp.where(even_w, 1, 2), jnp.where(even_w, 2, 1)
    up_z, down_z = jnp.where(even_z, 1, 2), jnp.where(even_z, 2, 1)
    sw = jnp.where(bi == 1, 0, jnp.where(bi == 2, up_w, down_w))
    sz = jnp.where(bj == 1, 0, jnp.where(bj == 2, up_z, down_z))
    head = jnp.where(sw == 0, atoms, w_base + (sw - 1) * 3 * bound)
    placed = head + sz * bound + (rel - block * bound)
    near = jnp.where(rel < 0, near, jnp.where(inside, placed, -1))
    near_ref[kpad - 8 :, :] = jnp.full((8, atoms), -1, I32)
    near_ref[0:1, :] = iota((1, atoms), 1)
    near_ref[1:slots, :] = near
    for c in range(3):
        for j in range(3):
            h = hessian_ref[c, j].astype(F32)
            h = jnp.concatenate([h, jnp.zeros((kpad - slots, atoms), F32)], axis=0)
            h = jnp.concatenate([h] * (atoms // kpad), axis=0)
            ht_ref[c * 3 + j] = h.T.astype(BF16)
    half = atoms // 2
    near = near_ref[...]
    for g in range(half // group):

        def store(c, j, hi, lo, g=g):
            for t, part in enumerate((hi, lo)):
                at = (t * 3 + c) * half + g * group
                m_ref[j, at : at + group, :] = part

        one_group(near, ht_ref, onehot_scr, store, g, group)


def second_kernel(
    m1_ref, near_ref, ht_ref, vectors_ref, labels_ref, masses_ref, rim_ref, ez_ref, oz_ref,
    m2_ref, product_ref, factor_ref, vt_ref,
    onehot_scr, local_scr, ext_scr,
):
    atoms, width = vectors_ref.shape[1:]
    bound = rim_ref.shape[1]
    w_base = ext_scr.shape[1]
    half = atoms // 2
    group = 16
    near = near_ref[...]
    for g in range(half // group):

        def store(c, j, hi, lo, g=g):
            for t, part in enumerate((hi, lo)):
                at = (t * 3 + c) * half + g * group
                local_scr[j, at : at + group, :] = part[:, :w_base]
                m2_ref[j, at : at + group, :] = part[:, w_base:]

        one_group(near, ht_ref, onehot_scr, store, g + half // group, group)
    factors = factor_rows(labels_ref[...], masses_ref[...])
    for v in range(2):
        f = jnp.broadcast_to(column(factors[v]), (atoms, width))
        factor_ref[v] = f
        for j in range(3):
            rows = vectors_ref[j].astype(F32) * f
            ext_scr[j, :atoms, v * width : (v + 1) * width] = rows.astype(BF16)
    scale_rows([rim_ref, ez_ref, oz_ref], ext_scr, atoms)
    used = atoms + 3 * bound
    for j in range(3):
        ext_scr[j, used:] = jnp.zeros((w_base - used, 2 * width), BF16)
        vt_ref[:, j * atoms : (j + 1) * atoms] = vectors_ref[j].astype(F32).T.astype(BF16)
    for h in range(2):
        total = 0.0
        for j in range(3):
            m = m1_ref[j, :, :w_base] if h == 0 else local_scr[j]
            total = total + dot(m, ext_scr[j])
        product_ref[h] = total[: 3 * half] + total[3 * half :]


def apply_kernel(
    m1_ref, m2_ref, product_ref, factor_ref, vt_ref, ew_ref, ow_ref,
    image_ref, mine_ref, other_ref, ext_scr,
):
    width, rows = vt_ref.shape
    atoms = rows // 3
    half = atoms // 2
    bound = ew_ref.shape[2]
    w_base = m1_ref.shape[2] - ext_scr.shape[1]
    scale_rows([ref.at[z] for ref in (ew_ref, ow_ref) for z in range(3)], ext_scr, 0)
    used = 6 * bound
    if used < ext_scr.shape[1]:
        for j in range(3):
            ext_scr[j, used:] = jnp.zeros((ext_scr.shape[1] - used, 2 * width), BF16)
    products = []
    for h in range(2):
        total = 0.0
        for j in range(3):
            m = m1_ref[j, :, w_base:] if h == 0 else m2_ref[j]
            total = total + dot(m, ext_scr[j])
        products.append(product_ref[h] + (total[: 3 * half] + total[3 * half :]))
    even = lax.rem(lax.axis_index("wide"), 2) == 0
    grams = []
    for v in range(2):
        parts = []
        for c in range(3):
            for h in range(2):
                block = products[h][c * half : (c + 1) * half, v * width : (v + 1) * width]
                parts.append(block * factor_ref[v, h * half : (h + 1) * half])
        image = jnp.concatenate(parts, axis=0)
        image_ref[v] = image
        hi, lo = split(image)
        grams.append(dot(vt_ref[...], hi) + dot(vt_ref[...], lo))
    mine_ref[...] = jnp.where(even, grams[0], grams[1])
    other_ref[...] = jnp.where(even, grams[1], grams[0])


def turn_kernel(image_ref, rotation_ref, out_ref):
    for v in range(2):
        hi, lo = split(image_ref[v])
        rhi, rlo = split(rotation_ref[v])
        out_ref[v] = dot(hi, rhi) + (dot(lo, rhi) + dot(hi, rlo))


def final_kernel(
    mine_ref, other_ref, turned_ref, vectors_ref, rotation_ref, gram_ref, out_ref, *, count
):
    atoms = vectors_ref.shape[1]
    even = lax.rem(lax.axis_index("wide"), 2) == 0
    mine, other = mine_ref[...] / count, other_ref[...] / count
    for v in range(2):
        gram = jnp.where(even, mine, other) if v == 0 else jnp.where(even, other, mine)
        gram_ref[v] = gram
        hi, lo = split(gram)
        rhi, rlo = split(rotation_ref[v])
        step = dot(hi, rhi) + (dot(lo, rhi) + dot(hi, rlo))
        shi, slo = split(step)
        for j in range(3):
            vec = vectors_ref[j]
            turned = turned_ref[v, j * atoms : (j + 1) * atoms]
            out_ref[v, j] = (turned - (dot(vec, shi) + dot(vec, slo))).astype(BF16)


def swap(array, n_wide, n_narrow, place):
    pairs = []
    for p in range(n_wide):
        for q in range(n_narrow):
            a, b = place(p, q)
            pairs.append((p * n_narrow + q, a * n_narrow + b))
    return lax.ppermute(array, AXES, pairs)


def odd_partner(i, n):
    k = i + 1 if i % 2 else i - 1
    return k if 0 <= k < n else None


def call(kernel, out, *args, scratch=(), cost=None, space=VMEM):
    shapes = [jax.ShapeDtypeStruct(s, d) for s, d in out]
    flops, moved = cost or (1000, 1000)
    return pl.pallas_call(
        kernel,
        out_shape=shapes,
        in_specs=[space] * len(args),
        out_specs=[VMEM] * len(shapes),
        scratch_shapes=list(scratch),
        compiler_params=pltpu.CompilerParams(vmem_limit_bytes=24 * 2**20),
        cost_estimate=pl.CostEstimate(flops=flops, bytes_accessed=moved, transcendentals=0),
    )(*args)


def local(vectors, hessian, neighbours, halo_atoms, labels, masses, rotation):
    n_wide = lax.axis_size("wide")
    n_narrow = lax.axis_size("narrow")
    atoms, width = vectors.shape[1:]
    bound = halo_atoms.shape[0]
    slots = hessian.shape[2]
    kpad = -(-slots // 64) * 64
    w_base = -(-(atoms + 3 * bound) // 128) * 128
    w_rows = -(-6 * bound // 128) * 128

    def exchange(array, place):
        return swap(array, n_wide, n_narrow, place)

    def odd_z(p, q):
        k = odd_partner(q, n_narrow)
        return (p ^ 1, q) if k is None else (p, k)

    def odd_w(p, q):
        k = odd_partner(p, n_wide)
        return (p, q ^ 1) if k is None else (k, q)

    raw = (
        vectors, halo_atoms.reshape(1, bound), labels.reshape(1, atoms), masses, neighbours,
        hessian, rotation,
    )
    raw = [pltpu.with_memory_space_constraint(a, pltpu.HBM) for a in raw]
    rim, vectors, labels, masses, near, hessian, rotation = call(
        prepare_kernel,
        [((4, bound, width), BF16)] + [(a.shape, a.dtype) for i, a in enumerate(raw) if i != 1],
        *raw,
        scratch=[pltpu.VMEM((1, bound), I32), pltpu.SemaphoreType.DMA((len(raw),))],
        space=pl.BlockSpec(memory_space=pltpu.HBM),
    )
    ez = exchange(rim, lambda p, q: (p, q ^ 1))
    oz = exchange(rim, odd_z)

    def first(*refs):
        first_kernel(*refs, n_wide=n_wide, n_narrow=n_narrow, bound=bound, w_base=w_base)

    cost = (9 * atoms * 16 * kpad * (w_base + w_rows), 4 * 2**20)
    onehot_scr = pltpu.VMEM((16 * kpad, w_base + w_rows), BF16)
    m1, near, ht = call(
        first,
        [
            ((3, 3 * atoms, w_base + w_rows), BF16),
            ((kpad, atoms), I32),
            ((9, atoms, atoms), BF16),
        ],
        near, hessian, scratch=[onehot_scr], cost=cost,
    )
    ez, oz, m1 = lax.optimization_barrier((ez, oz, m1))
    three = jnp.stack([rim, ez, oz])
    ew = exchange(three, lambda p, q: (p ^ 1, q))
    ow = exchange(three, odd_w)
    m2, product, factor, vt = call(
        second_kernel,
        [
            ((3, 3 * atoms, w_rows), BF16),
            ((2, 3 * atoms // 2, 2 * width), F32),
            ((2, atoms, width), F32),
            ((width, 3 * atoms), BF16),
        ],
        m1, near, ht, vectors, labels, masses, rim, ez, oz,
        scratch=[
            onehot_scr,
            pltpu.VMEM((3, 3 * atoms, w_base), BF16),
            pltpu.VMEM((3, w_base, 2 * width), BF16),
        ],
        cost=cost,
    )
    image, mine, other = call(
        apply_kernel,
        [((2, 3 * atoms, width), F32), ((width, width), F32), ((width, width), F32)],
        m1, m2, product, factor, vt, ew, ow,
        scratch=[pltpu.VMEM((3, w_rows, 2 * width), BF16)],
        cost=(2 * 18 * atoms * w_rows * 2 * width, 4 * 2**20),
    )
    (turned,) = call(
        turn_kernel, [((2, 3 * atoms, width), F32)], image, rotation,
        cost=(2 * 18 * atoms * width * width, 2**20),
    )
    total = mine + exchange(other, lambda p, q: (p ^ 1, q))
    bits = [(1 << k, 0) for k in range(1, n_wide.bit_length() - 1)]
    bits += [(0, 1 << k) for k in range(n_narrow.bit_length() - 1)]
    for k in range(0, len(bits), 2):
        steps = list(bits[k : k + 2])
        if len(steps) == 2:
            steps.insert(0, (steps[0][0] ^ steps[1][0], steps[0][1] ^ steps[1][1]))
        parts = [exchange(total, lambda p, q, s=s: (p ^ s[0], q ^ s[1])) for s in steps]
        for part in parts:
            total = total + part
    other = exchange(total, lambda p, q: (p ^ 1, q))
    count = 3.0 * atoms * n_wide * n_narrow

    def final(*refs):
        final_kernel(*refs, count=count)

    gram, rotated = call(
        final,
        [((2, width, width), F32), ((2, 3, atoms, width), BF16)],
        total, other, turned, vectors, rotation,
    )
    return gram, rotated


def solution(mesh):
    for size in mesh.shape.values():
        assert size & (size - 1) == 0 and size > 1
    return jax.shard_map(
        local,
        mesh=mesh,
        in_specs=(
            P(None, AXES, None),
            P(None, None, None, AXES),
            P(None, AXES),
            P(AXES),
            P(AXES),
            P(),
            P(),
        ),
        out_specs=(P(), P(None, None, AXES, None)),
        check_vma=False,
    )
```

time: 41.4 us -> 35.6 us (0.86)
  local copies, waits for them, and re-layouts: 5.88 us -> 0 us
  waiting for transfers between devices: 11.7 us -> 13.4 us
  Pallas kernels: 7.3 us -> 6.32 us
    unnamed x18 -> x0, local copies, waits for them, and re-layouts: 5.88 us -> none
    ppermute x12, waiting for transfers between devices: 11.7 us -> 13.4 us  [swap(): return lax.ppermute(array, AXES, pairs)]
    pallas_call x5 -> x6, Pallas kernels: 7.3 us -> 6.32 us  [call(): pl.pallas_call(kernel, out_shape=shapes, in_specs=[space] * len(args), ou...]
    ppermute x12, starting transfers between devices: 15.4 us -> 15 us  [swap(): return lax.ppermute(array, AXES, pairs)]
  transfers between devices with their start and end apart: 12 -> 12, of which waited for: 8 -> 10; matrix products, arithmetic and copies ran while one was open for 0% -> 0% of each run, Pallas kernels for 11% -> 8%
where the time goes in v2:
time: 35.6 us; the launch traced here: 35.4 us
  starting transfers between devices  15 us (42%)
  waiting for transfers between devices  13.4 us (38%)
  Pallas kernels  6.32 us (18%)
  between operations  0.72 us (2%)
    ppermute x12, starting transfers between devices, swap(): return lax.ppermute(array, AXES, pairs)  15 us
    ppermute x12, waiting for transfers between devices, swap(): return lax.ppermute(array, AXES, pairs)  13.4 us
    pallas_call x6, Pallas kernels, call(): pl.pallas_call(kernel, out_shape=shapes, in_specs=[space] * len(args), ou...  6.32 us
  transfers between devices with their start and end apart: 12, of which 10 were waited for; matrix products, arithmetic and copies ran while one was open for 0% of the time, Pallas kernels for 8%

profile of v2, /device:TPU:0, one launch (start us, length us, event | category | flops | bytes accessed | tf_op | source)
XLA Modules:
  0.0 35.4 jit_solution(4183245387368417884)
XLA Ops:
  0.6 1.2 %shard_map.86 = (bf16[4,32,128]{2,1,0:T(8,128)(2,1)S(1)}, bf16[3,128,128]{2,1,0:T(8,128)(2,1)S(1)}, s32[1,128]{1,0:T(1,128)S(1)}, f32[2,16]{1,0:T(2,128)S(1)}, s...) custom-call(bf16[3,128,128]{2,1,0:T(8,128)(2,1)} %vectors_hbm.1, ...), custom_call_target="tpu_custom_call" | custom-call | flops 1000 | bytes 1000 | tf_op jit(solution)/shard_map/pallas_call | solution.py:277
  1.8 0.6 %collective-permute-start.1 = (bf16[4,32,128]{2,1,0:T(8,128)(2,1)S(1)}, bf16[4,32,128]{2,1,0:T(8,128)(2,1)S(1)}, u32[]{:S(2)}, u32[]{:S(2)}) collective-permute-start(bf16[4,32,128]{2,1,0:T(8,128)(2,1)S(1)} %get-tuple-element.22.rim_ref), channel_id=1, source_target_pairs={{0,4},{1,2},{2,1},{3,7},{4,0},{5,6},{6,5},{7,3},{8,12},{9,10},{10,... | collective-permute-start | bytes 98312 | tf_op jit(solution)/shard_map/ppermute | solution.py:266
  2.4 4.1 %collective-permute-start = (bf16[4,32,128]{2,1,0:T(8,128)(2,1)S(1)}, bf16[4,32,128]{2,1,0:T(8,128)(2,1)S(1)}, u32[]{:S(2)}, u32[]{:S(2)}) collective-permute-start(bf16[4,32,128]{2,1,0:T(8,128)(2,1)S(1)} %get-tuple-element.22.rim_ref), channel_id=1, source_target_pairs={{0,1},{1,0},{2,3},{3,2},{4,5},{5,4},{6,7},{7,6},{8,9},{9,8},{10,11... | collective-permute-start | bytes 98312 | tf_op jit(solution)/shard_map/ppermute | solution.py:266
  6.5 1.1 %shard_map.87 = (bf16[3,384,512]{2,1,0:T(8,128)(2,1)S(1)}, s32[64,128]{1,0:T(8,128)S(1)}, bf16[9,128,128]{2,1,0:T(8,128)(2,1)S(1)}) custom-call(s32[60,128]{1,0:T(8,128)S(1)} %get-tuple-element.23.refs_0_, bf16[3,3,61,128]{3,2,1,0:T(8,128)(2,1)S(1)} %get-tuple-element.24.refs_1_), custom_call_target="tpu_custom_call" | custom-call | flops 603979776 | bytes 4194304 | tf_op jit(solution)/shard_map/pallas_call | solution.py:277
  7.7 0.0 collective-permute-done.1.oz_ref
  7.7 0.7 %collective-permute-done.ez_ref = bf16[4,32,128]{2,1,0:T(8,128)(2,1)S(1)} collective-permute-done((bf16[4,32,128]{2,1,0:T(8,128)(2,1)S(1)}, bf16[4,32,128]{2,1,0:T(8,128)(2,1)S(1)}, u32[]{:S(2)}, u32[]{:S(2)}) %collective-permute-start) | collective-permute-done | bytes 32800 | tf_op jit(solution)/shard_map/ppermute | solution.py:266
  8.4 2.1 %collective-permute-start.3 = (bf16[3,4,32,128]{3,2,1,0:T(8,128)(2,1)S(1)}, bf16[3,4,32,128]{3,2,1,0:T(8,128)(2,1)S(1)}, u32[]{:S(2)}, u32[]{:S(2)}) collective-permute-start(bf16[3,4,32,128]{3,2,1,0:T(8,128)(2,1)S(1)} %pad_maximum_fusion), channel_id=1, source_target_pairs={{0,1},{1,0},{2,3},{3,2},{4,8},{5,9},{6,10},{7,11},{8,4},{9,5},{10,... | collective-permute-start | bytes 294920 | tf_op jit(solution)/shard_map/ppermute | solution.py:266
  10.5 0.0 collective-permute-start.2
  10.5 1.5 %shard_map.88 = (bf16[3,384,256]{2,1,0:T(8,128)(2,1)S(1)}, f32[2,192,256]{2,1,0:T(8,128)S(1)}, f32[2,128,128]{2,1,0:T(8,128)S(1)}, bf16[128,384]{1,0:T(8,128)(2,1)S(1)}) custom-call(bf16[3,384,512]{2,1,0:T(8,128)(2,1)S(1)} %get-tuple-element.26.m1_ref, s32[64,128]{1,0:T(8,128)S(1)} %get-tuple-element.27.near_ref, ...), custom_call_target="tpu_custom_call" | custom-call | flops 603979776 | bytes 4194304 | tf_op jit(solution)/shard_map/pallas_call | solution.py:277
  12.0 1.1 %collective-permute-done.3.ow_ref = bf16[3,4,32,128]{3,2,1,0:T(8,128)(2,1)S(1)} collective-permute-done((bf16[3,4,32,128]{3,2,1,0:T(8,128)(2,1)S(1)}, bf16[3,4,32,128]{3,2,1,0:T(8,128)(2,1)S(1)}, u32[]{:S(2)}, u32[]{:S(2)}) %collective-permute-start.3) | collective-permute-done | bytes 98336 | tf_op jit(solution)/shard_map/ppermute | solution.py:266
  13.1 0.0 collective-permute-done.2.ew_ref
  13.1 0.9 %shard_map.89 = (f32[2,384,128]{2,1,0:T(8,128)S(1)}, f32[128,128]{1,0:T(8,128)S(1)}, f32[128,128]{1,0:T(8,128)S(1)}) custom-call(bf16[3,384,512]{2,1,0:T(8,128)(2,1)S(1)} %get-tuple-element.26.m1_ref, bf16[3,384,256]{2,1,0:T(8,128)(2,1)S(1)} %get-tuple-element.34.m2_ref, f32[2,192,256]{2,1,0:T(8,128)S(1)} %get-tuple-element.35.product_ref, ...), custom_call_target="tpu_custom_call" | custom-call | flops 301989888 | bytes 4194304 | tf_op jit(solution)/shard_map/pallas_call | solution.py:277
  14.0 0.1 collective-permute-start.4
  14.1 1.2 %collective-permute-done.4 = f32[128,128]{1,0:T(8,128)S(1)} collective-permute-done((f32[128,128]{1,0:T(8,128)S(1)}, f32[128,128]{1,0:T(8,128)S(1)}, u32[]{:S(2)}, u32[]{:S(2)}) %collective-permute-start.4) | collective-permute-done | bytes 65568 | tf_op jit(solution)/shard_map/ppermute | solution.py:266
  15.4 2.0 %collective-permute-start.7 = (f32[128,128]{1,0:T(8,128)S(1)}, f32[128,128]{1,0:T(8,128)S(1)}, u32[]{:S(2)}, u32[]{:S(2)}) collective-permute-start(f32[128,128]{1,0:T(8,128)S(1)} %add.21), channel_id=1, source_target_pairs={{0,16},{1,17},{2,18},{3,19},{4,20},{5,21},{6,22},{7,23},{8,24},{9,... | collective-permute-start | bytes 196616 | tf_op jit(solution)/shard_map/ppermute | solution.py:266
  17.4 0.6 %collective-permute-start.6 = (f32[128,128]{1,0:T(8,128)S(1)}, f32[128,128]{1,0:T(8,128)S(1)}, u32[]{:S(2)}, u32[]{:S(2)}) collective-permute-start(f32[128,128]{1,0:T(8,128)S(1)} %add.21), channel_id=1, source_target_pairs={{0,8},{1,9},{2,10},{3,11},{4,12},{5,13},{6,14},{7,15},{8,0},{9,1},... | collective-permute-start | bytes 196616 | tf_op jit(solution)/shard_map/ppermute | solution.py:266
  18.0 0.9 %collective-permute-start.5 = (f32[128,128]{1,0:T(8,128)S(1)}, f32[128,128]{1,0:T(8,128)S(1)}, u32[]{:S(2)}, u32[]{:S(2)}) collective-permute-start(f32[128,128]{1,0:T(8,128)S(1)} %add.21), channel_id=1, source_target_pairs={{0,24},{1,25},{2,26},{3,27},{4,28},{5,29},{6,30},{7,31},{8,16},{9,... | collective-permute-start | bytes 196616 | tf_op jit(solution)/shard_map/ppermute | solution.py:266
  19.0 0.9 %collective-permute-done.7 = f32[128,128]{1,0:T(8,128)S(1)} collective-permute-done((f32[128,128]{1,0:T(8,128)S(1)}, f32[128,128]{1,0:T(8,128)S(1)}, u32[]{:S(2)}, u32[]{:S(2)}) %collective-permute-start.7) | collective-permute-done | bytes 65568 | tf_op jit(solution)/shard_map/ppermute | solution.py:266
  19.8 2.2 %collective-permute-done.6 = f32[128,128]{1,0:T(8,128)S(1)} collective-permute-done((f32[128,128]{1,0:T(8,128)S(1)}, f32[128,128]{1,0:T(8,128)S(1)}, u32[]{:S(2)}, u32[]{:S(2)}) %collective-permute-start.6) | collective-permute-done | bytes 65568 | tf_op jit(solution)/shard_map/ppermute | solution.py:266
  22.0 1.2 %collective-permute-done.5 = f32[128,128]{1,0:T(8,128)S(1)} collective-permute-done((f32[128,128]{1,0:T(8,128)S(1)}, f32[128,128]{1,0:T(8,128)S(1)}, u32[]{:S(2)}, u32[]{:S(2)}) %collective-permute-start.5) | collective-permute-done | bytes 65568 | tf_op jit(solution)/shard_map/ppermute | solution.py:266
  23.2 2.0 %collective-permute-start.10 = (f32[128,128]{1,0:T(8,128)S(1)}, f32[128,128]{1,0:T(8,128)S(1)}, u32[]{:S(2)}, u32[]{:S(2)}) collective-permute-start(f32[128,128]{1,0:T(8,128)S(1)} %add_add_fusion.1), channel_id=1, source_target_pairs={{0,2},{1,3},{2,0},{3,1},{4,6},{5,7},{6,4},{7,5},{8,10},{9,11},{10,... | collective-permute-start | bytes 196616 | tf_op jit(solution)/shard_map/ppermute | solution.py:266
  25.2 1.5 %collective-permute-start.9 = (f32[128,128]{1,0:T(8,128)S(1)}, f32[128,128]{1,0:T(8,128)S(1)}, u32[]{:S(2)}, u32[]{:S(2)}) collective-permute-start(f32[128,128]{1,0:T(8,128)S(1)} %add_add_fusion.1), channel_id=1, source_target_pairs={{0,1},{1,0},{2,3},{3,2},{4,5},{5,4},{6,7},{7,6},{8,9},{9,8},{10,11... | collective-permute-start | bytes 196616 | tf_op jit(solution)/shard_map/ppermute | solution.py:266
  26.7 1.0 %collective-permute-start.8 = (f32[128,128]{1,0:T(8,128)S(1)}, f32[128,128]{1,0:T(8,128)S(1)}, u32[]{:S(2)}, u32[]{:S(2)}) collective-permute-start(f32[128,128]{1,0:T(8,128)S(1)} %add_add_fusion.1), channel_id=1, source_target_pairs={{0,3},{1,2},{2,1},{3,0},{4,7},{5,6},{6,5},{7,4},{8,11},{9,10},{10,... | collective-permute-start | bytes 196616 | tf_op jit(solution)/shard_map/ppermute | solution.py:266
  27.6 1.2 %collective-permute-done.10 = f32[128,128]{1,0:T(8,128)S(1)} collective-permute-done((f32[128,128]{1,0:T(8,128)S(1)}, f32[128,128]{1,0:T(8,128)S(1)}, u32[]{:S(2)}, u32[]{:S(2)}) %collective-permute-start.10) | collective-permute-done | bytes 65568 | tf_op jit(solution)/shard_map/ppermute | solution.py:266
  28.9 1.4 %collective-permute-done.9 = f32[128,128]{1,0:T(8,128)S(1)} collective-permute-done((f32[128,128]{1,0:T(8,128)S(1)}, f32[128,128]{1,0:T(8,128)S(1)}, u32[]{:S(2)}, u32[]{:S(2)}) %collective-permute-start.9) | collective-permute-done | bytes 65568 | tf_op jit(solution)/shard_map/ppermute | solution.py:266
  30.3 2.5 %collective-permute-done.8 = f32[128,128]{1,0:T(8,128)S(1)} collective-permute-done((f32[128,128]{1,0:T(8,128)S(1)}, f32[128,128]{1,0:T(8,128)S(1)}, u32[]{:S(2)}, u32[]{:S(2)}) %collective-permute-start.8) | collective-permute-done | bytes 65568 | tf_op jit(solution)/shard_map/ppermute | solution.py:266
  32.8 0.1 collective-permute-start.11
  32.9 0.3 shard_map.90.refs_2_
  33.2 0.9 %collective-permute-done.11.refs_1_ = f32[128,128]{1,0:T(8,128)S(1)} collective-permute-done((f32[128,128]{1,0:T(8,128)S(1)}, f32[128,128]{1,0:T(8,128)S(1)}, u32[]{:S(2)}, u32[]{:S(2)}) %collective-permute-start.11) | collective-permute-done | bytes 65568 | tf_op jit(solution)/shard_map/ppermute | solution.py:266
  34.1 1.3 %shard_map.91 = (f32[2,128,128]{2,1,0:T(8,128)}, bf16[2,3,128,128]{3,2,1,0:T(8,128)(2,1)}) custom-call(f32[128,128]{1,0:T(8,128)S(1)} %add_add_fusion.refs_0_, f32[128,128]{1,0:T(8,128)S(1)} %collective-permute-done.11.refs_1_, f32[2,384,128]{2,1,0:T(8,128)S(1)} %shard_map.90.refs_2_, bf16[3,128,128]{2,1,0:T(8,128)(2,1)S(1)} %get-tuple-element.29.vectors_ref.refs_3_, ...), custom_call_target="tpu_custom_call" | custom-call | flops 1000 | bytes 1000 | tf_op jit(solution)/shard_map/pallas_call | solution.py:277
  (4 shorter events, 0.1 us)
Async XLA Ops:
  1.8 5.8 %collective-permute-start.1 = (bf16[4,32,128]{2,1,0:T(8,128)(2,1)S(1)}, bf16[4,32,128]{2,1,0:T(8,128)(2,1)S(1)}, u32[]{:S(2)}, u32[]{:S(2)}) collective-permute-start(bf16[4,32,128]{2,1,0:T(8,128)(2,1)S(1)} %get-tuple-element.22.rim_ref), channel_id=1, source_target_pairs={{0,4},{1,2},{2,1},{3,7},{4,0},{5,6},{6,5},{7,3},{8,12},{9,10},{10,... | collective-permute-start | bytes 98312 | tf_op jit(solution)/shard_map/ppermute | solution.py:266
  2.4 6.0 %collective-permute-start = (bf16[4,32,128]{2,1,0:T(8,128)(2,1)S(1)}, bf16[4,32,128]{2,1,0:T(8,128)(2,1)S(1)}, u32[]{:S(2)}, u32[]{:S(2)}) collective-permute-start(bf16[4,32,128]{2,1,0:T(8,128)(2,1)S(1)} %get-tuple-element.22.rim_ref), channel_id=1, source_target_pairs={{0,1},{1,0},{2,3},{3,2},{4,5},{5,4},{6,7},{7,6},{8,9},{9,8},{10,11... | collective-permute-start | bytes 98312 | tf_op jit(solution)/shard_map/ppermute | solution.py:266
  8.4 4.7 %collective-permute-start.3 = (bf16[3,4,32,128]{3,2,1,0:T(8,128)(2,1)S(1)}, bf16[3,4,32,128]{3,2,1,0:T(8,128)(2,1)S(1)}, u32[]{:S(2)}, u32[]{:S(2)}) collective-permute-start(bf16[3,4,32,128]{3,2,1,0:T(8,128)(2,1)S(1)} %pad_maximum_fusion), channel_id=1, source_target_pairs={{0,1},{1,0},{2,3},{3,2},{4,8},{5,9},{6,10},{7,11},{8,4},{9,5},{10,... | collective-permute-start | bytes 294920 | tf_op jit(solution)/shard_map/ppermute | solution.py:266
  10.5 2.6 %collective-permute-start.2 = (bf16[3,4,32,128]{3,2,1,0:T(8,128)(2,1)S(1)}, bf16[3,4,32,128]{3,2,1,0:T(8,128)(2,1)S(1)}, u32[]{:S(2)}, u32[]{:S(2)}) collective-permute-start(bf16[3,4,32,128]{3,2,1,0:T(8,128)(2,1)S(1)} %pad_maximum_fusion), channel_id=1, source_target_pairs={{0,4},{1,5},{2,6},{3,7},{4,0},{5,1},{6,2},{7,3},{8,12},{9,13},{10,... | collective-permute-start | bytes 294920 | tf_op jit(solution)/shard_map/ppermute | solution.py:266
  14.0 1.3 %collective-permute-start.4 = (f32[128,128]{1,0:T(8,128)S(1)}, f32[128,128]{1,0:T(8,128)S(1)}, u32[]{:S(2)}, u32[]{:S(2)}) collective-permute-start(f32[128,128]{1,0:T(8,128)S(1)} %get-tuple-element.39), channel_id=1, source_target_pairs={{0,4},{1,5},{2,6},{3,7},{4,0},{5,1},{6,2},{7,3},{8,12},{9,13},{10,... | collective-permute-start | bytes 196616 | tf_op jit(solution)/shard_map/ppermute | solution.py:266
  15.4 4.5 %collective-permute-start.7 = (f32[128,128]{1,0:T(8,128)S(1)}, f32[128,128]{1,0:T(8,128)S(1)}, u32[]{:S(2)}, u32[]{:S(2)}) collective-permute-start(f32[128,128]{1,0:T(8,128)S(1)} %add.21), channel_id=1, source_target_pairs={{0,16},{1,17},{2,18},{3,19},{4,20},{5,21},{6,22},{7,23},{8,24},{9,... | collective-permute-start | bytes 196616 | tf_op jit(solution)/shard_map/ppermute | solution.py:266
  17.4 4.6 %collective-permute-start.6 = (f32[128,128]{1,0:T(8,128)S(1)}, f32[128,128]{1,0:T(8,128)S(1)}, u32[]{:S(2)}, u32[]{:S(2)}) collective-permute-start(f32[128,128]{1,0:T(8,128)S(1)} %add.21), channel_id=1, source_target_pairs={{0,8},{1,9},{2,10},{3,11},{4,12},{5,13},{6,14},{7,15},{8,0},{9,1},... | collective-permute-start | bytes 196616 | tf_op jit(solution)/shard_map/ppermute | solution.py:266
  18.0 5.2 %collective-permute-start.5 = (f32[128,128]{1,0:T(8,128)S(1)}, f32[128,128]{1,0:T(8,128)S(1)}, u32[]{:S(2)}, u32[]{:S(2)}) collective-permute-start(f32[128,128]{1,0:T(8,128)S(1)} %add.21), channel_id=1, source_target_pairs={{0,24},{1,25},{2,26},{3,27},{4,28},{5,29},{6,30},{7,31},{8,16},{9,... | collective-permute-start | bytes 196616 | tf_op jit(solution)/shard_map/ppermute | solution.py:266
  23.2 5.7 %collective-permute-start.10 = (f32[128,128]{1,0:T(8,128)S(1)}, f32[128,128]{1,0:T(8,128)S(1)}, u32[]{:S(2)}, u32[]{:S(2)}) collective-permute-start(f32[128,128]{1,0:T(8,128)S(1)} %add_add_fusion.1), channel_id=1, source_target_pairs={{0,2},{1,3},{2,0},{3,1},{4,6},{5,7},{6,4},{7,5},{8,10},{9,11},{10,... | collective-permute-start | bytes 196616 | tf_op jit(solution)/shard_map/ppermute | solution.py:266
  25.2 5.1 %collective-permute-start.9 = (f32[128,128]{1,0:T(8,128)S(1)}, f32[128,128]{1,0:T(8,128)S(1)}, u32[]{:S(2)}, u32[]{:S(2)}) collective-permute-start(f32[128,128]{1,0:T(8,128)S(1)} %add_add_fusion.1), channel_id=1, source_target_pairs={{0,1},{1,0},{2,3},{3,2},{4,5},{5,4},{6,7},{7,6},{8,9},{9,8},{10,11... | collective-permute-start | bytes 196616 | tf_op jit(solution)/shard_map/ppermute | solution.py:266
  26.7 6.1 %collective-permute-start.8 = (f32[128,128]{1,0:T(8,128)S(1)}, f32[128,128]{1,0:T(8,128)S(1)}, u32[]{:S(2)}, u32[]{:S(2)}) collective-permute-start(f32[128,128]{1,0:T(8,128)S(1)} %add_add_fusion.1), channel_id=1, source_target_pairs={{0,3},{1,2},{2,1},{3,0},{4,7},{5,6},{6,5},{7,4},{8,11},{9,10},{10,... | collective-permute-start | bytes 196616 | tf_op jit(solution)/shard_map/ppermute | solution.py:266
  32.8 1.3 %collective-permute-start.11 = (f32[128,128]{1,0:T(8,128)S(1)}, f32[128,128]{1,0:T(8,128)S(1)}, u32[]{:S(2)}, u32[]{:S(2)}) collective-permute-start(f32[128,128]{1,0:T(8,128)S(1)} %add_add_fusion.refs_0_), channel_id=1, source_target_pairs={{0,4},{1,5},{2,6},{3,7},{4,0},{5,1},{6,2},{7,3},{8,12},{9,13},{10,... | collective-permute-start | bytes 196616 | tf_op jit(solution)/shard_map/ppermute | solution.py:266

commit v3 on v2

--- a/solution.py
+++ b/solution.py
@@ -1,3 +1,5 @@
+import functools
+
 import jax
 import jax.numpy as jnp
 from jax import lax
@@ -75,7 +77,7 @@
         copy.wait()
 
 
-def scale_rows(blocks, ext_ref, base):
+def scale_rows(blocks, exts, base):
     bound, width = blocks[0].shape[1:]
     count = bound * len(blocks)
     shape = (width, 2 * width)
@@ -84,7 +86,7 @@
     for j in range(3):
         rows = jnp.concatenate([b[j] for b in blocks], axis=0).astype(F32)
         rows = jnp.concatenate([rows, rows], axis=1) * factor
-        ext_ref[j, base : base + count] = rows.astype(BF16)
+        exts[j][base : base + count] = rows.astype(BF16)
 
 
 def one_group(near, ht_ref, onehot_scr, store, g, group):
@@ -154,10 +156,21 @@
         one_group(near, ht_ref, onehot_scr, store, g, group)
 
 
+def scaled_image(products, factor_ref, v):
+    half = products[0].shape[0] // 3
+    width = products[0].shape[1] // 2
+    parts = []
+    for h in range(2):
+        for c in range(3):
+            block = products[h][c * half : (c + 1) * half, v * width : (v + 1) * width]
+            parts.append(block * factor_ref[v, h * half : (h + 1) * half])
+    return jnp.concatenate(parts, axis=0)
+
+
 def second_kernel(
     m1_ref, near_ref, ht_ref, vectors_ref, labels_ref, masses_ref, rim_ref, ez_ref, oz_ref,
-    m2_ref, product_ref, factor_ref, vt_ref,
-    onehot_scr, local_scr, ext_scr,
+    m2_ref, product_ref, factor_ref, gram_ref, reach_ref,
+    onehot_scr, local_scr, ext_scr, vt_scr,
 ):
     atoms, width = vectors_ref.shape[1:]
     bound = rim_ref.shape[1]
@@ -181,80 +194,115 @@
         for j in range(3):
             rows = vectors_ref[j].astype(F32) * f
             ext_scr[j, :atoms, v * width : (v + 1) * width] = rows.astype(BF16)
-    scale_rows([rim_ref, ez_ref, oz_ref], ext_scr, atoms)
+    scale_rows([rim_ref, ez_ref, oz_ref], [ext_scr.at[j] for j in range(3)], atoms)
     used = atoms + 3 * bound
     for j in range(3):
         ext_scr[j, used:] = jnp.zeros((w_base - used, 2 * width), BF16)
-        vt_ref[:, j * atoms : (j + 1) * atoms] = vectors_ref[j].astype(F32).T.astype(BF16)
+        turned = vectors_ref[j].astype(F32).T
+        for h in range(2):
+            at = (3 * h + j) * half
+            vt_scr[:, at : at + half] = turned[:, h * half : (h + 1) * half]
+    products = []
     for h in range(2):
         total = 0.0
         for j in range(3):
             m = m1_ref[j, :, :w_base] if h == 0 else local_scr[j]
             total = total + dot(m, ext_scr[j])
-        product_ref[h] = total[: 3 * half] + total[3 * half :]
-
-
-def apply_kernel(
-    m1_ref, m2_ref, product_ref, factor_ref, vt_ref, ew_ref, ow_ref,
-    image_ref, mine_ref, other_ref, ext_scr,
-):
-    width, rows = vt_ref.shape
-    atoms = rows // 3
-    half = atoms // 2
-    bound = ew_ref.shape[2]
-    w_base = m1_ref.shape[2] - ext_scr.shape[1]
-    scale_rows([ref.at[z] for ref in (ew_ref, ow_ref) for z in range(3)], ext_scr, 0)
+        products.append(total[: 3 * half] + total[3 * half :])
+        product_ref[h] = products[h]
+    vt = vt_scr[...]
+    for v in range(2):
+        hi, lo = split(scaled_image(products, factor_ref, v))
+        both = dot(vt.astype(BF16), jnp.concatenate([hi, lo], axis=1))
+        gram_ref[v] = both[:, :width] + both[:, width:]
+    scaled = []
+    for v in range(2):
+        row = factors[v]
+        cols = [row[:, h * half : (h + 1) * half] for h in range(2) for c in range(3)]
+        scaled.append(vt * jnp.concatenate(cols, axis=1))
+    fhi, flo = split(jnp.concatenate(scaled, axis=0))
+    for j in range(3):
+        total = 0.0
+        for h in range(2):
+            at = slice(3 * h * half, 3 * (h + 1) * half)
+            left = jnp.concatenate([fhi[:, at], flo[:, at]], axis=0)
+            m = m1_ref[j, :, w_base:] if h == 0 else m2_ref[j]
+            high = dot(left, m[: 3 * half])
+            low = dot(fhi[:, at], m[3 * half :])
+            total = total + (high[: 2 * width] + (high[2 * width :] + low))
+        cols = total.shape[1]
+        hi, lo = split(total)
+        for v in range(2):
+            rows = slice(v * width, (v + 1) * width)
+            reach_ref[v, :, j * cols : (j + 1) * cols] = hi[rows]
+            reach_ref[v, :, (3 + j) * cols : (4 + j) * cols] = lo[rows]
+
+
+def partial_kernel(reach_ref, gram_ref, ew_ref, ow_ref, mine_ref, other_ref, ext_ref):
+    bound, width = ew_ref.shape[2:]
+    rows = ext_ref.shape[0] // 3
     used = 6 * bound
-    if used < ext_scr.shape[1]:
+    blocks = [ref.at[z] for ref in (ew_ref, ow_ref) for z in range(3)]
+    scale_rows(blocks, [ext_ref.at[j * rows : (j + 1) * rows] for j in range(3)], 0)
+    if used < rows:
         for j in range(3):
-            ext_scr[j, used:] = jnp.zeros((ext_scr.shape[1] - used, 2 * width), BF16)
+            ext_ref[j * rows + used : (j + 1) * rows] = jnp.zeros((rows - used, 2 * width), BF16)
+    even = lax.rem(lax.axis_index("wide"), 2) == 0
+    grams = []
+    for v in range(2):
+        ext = ext_ref[:, v * width : (v + 1) * width]
+        hi, lo = reach_ref[v, :, : 3 * rows], reach_ref[v, :, 3 * rows :]
+        grams.append(gram_ref[v] + (dot(hi, ext) + dot(lo, ext)))
+    mine_ref[...] = jnp.where(even, grams[0], grams[1])
+    other_ref[...] = jnp.where(even, grams[1], grams[0])
+
+
+def turn_kernel(m1_ref, m2_ref, product_ref, factor_ref, ext_ref, rotation_ref, out_ref):
+    half = factor_ref.shape[1] // 2
+    width = factor_ref.shape[2]
+    rows = ext_ref.shape[0] // 3
+    w_base = m1_ref.shape[2] - rows
     products = []
     for h in range(2):
         total = 0.0
         for j in range(3):
             m = m1_ref[j, :, w_base:] if h == 0 else m2_ref[j]
-            total = total + dot(m, ext_scr[j])
+            total = total + dot(m, ext_ref[j * rows : (j + 1) * rows])
         products.append(product_ref[h] + (total[: 3 * half] + total[3 * half :]))
-    even = lax.rem(lax.axis_index("wide"), 2) == 0
-    grams = []
-    for v in range(2):
-        parts = []
-        for c in range(3):
-            for h in range(2):
-                block = products[h][c * half : (c + 1) * half, v * width : (v + 1) * width]
-                parts.append(block * factor_ref[v, h * half : (h + 1) * half])
-        image = jnp.concatenate(parts, axis=0)
-        image_ref[v] = image
-        hi, lo = split(image)
-        grams.append(dot(vt_ref[...], hi) + dot(vt_ref[...], lo))
-    mine_ref[...] = jnp.where(even, grams[0], grams[1])
-    other_ref[...] = jnp.where(even, grams[1], grams[0])
-
-
-def turn_kernel(image_ref, rotation_ref, out_ref):
-    for v in range(2):
-        hi, lo = split(image_ref[v])
+    for v in range(2):
+        hi, lo = split(scaled_image(products, factor_ref, v))
         rhi, rlo = split(rotation_ref[v])
-        out_ref[v] = dot(hi, rhi) + (dot(lo, rhi) + dot(hi, rlo))
-
-
-def final_kernel(
-    mine_ref, other_ref, turned_ref, vectors_ref, rotation_ref, gram_ref, out_ref, *, count
+        both = dot(hi, jnp.concatenate([rhi, rlo], axis=1))
+        res = both[:, :width] + (both[:, width:] + dot(lo, rhi))
+        for h in range(2):
+            for c in range(3):
+                at = (2 * c + h) * half
+                out_ref[v, at : at + half] = res[(3 * h + c) * half : (3 * h + c + 1) * half]
+
+
+def finish_kernel(
+    total_ref, turned_ref, vectors_ref, rotation_ref, *refs, count, own
 ):
+    gram_hbm, out_hbm, gram_scr, out_scr, sems = refs[-5:]
     atoms = vectors_ref.shape[1]
-    even = lax.rem(lax.axis_index("wide"), 2) == 0
-    mine, other = mine_ref[...] / count, other_ref[...] / count
-    for v in range(2):
-        gram = jnp.where(even, mine, other) if v == 0 else jnp.where(even, other, mine)
-        gram_ref[v] = gram
-        hi, lo = split(gram)
-        rhi, rlo = split(rotation_ref[v])
-        step = dot(hi, rhi) + (dot(lo, rhi) + dot(hi, rlo))
-        shi, slo = split(step)
-        for j in range(3):
-            vec = vectors_ref[j]
-            turned = turned_ref[v, j * atoms : (j + 1) * atoms]
-            out_ref[v, j] = (turned - (dot(vec, shi) + dot(vec, slo))).astype(BF16)
+    v = lax.rem(lax.axis_index("wide"), 2)
+    v = v if own else 1 - v
+    gram = total_ref[...] / count
+    gram_scr[...] = gram
+    first = pltpu.make_async_copy(gram_scr, gram_hbm.at[v], sems.at[0])
+    first.start()
+    hi, lo = split(gram)
+    rhi, rlo = split(rotation_ref[v])
+    step = dot(hi, rhi) + (dot(lo, rhi) + dot(hi, rlo))
+    shi, slo = split(step)
+    for j in range(3):
+        vec = vectors_ref[j]
+        turned = turned_ref[v, j * atoms : (j + 1) * atoms]
+        out_scr[j] = (turned - (dot(vec, shi) + dot(vec, slo))).astype(BF16)
+    second = pltpu.make_async_copy(out_scr, out_hbm.at[v], sems.at[1])
+    second.start()
+    first.wait()
+    second.wait()
 
 
 def swap(array, n_wide, n_narrow, place):
@@ -339,32 +387,33 @@
     three = jnp.stack([rim, ez, oz])
     ew = exchange(three, lambda p, q: (p ^ 1, q))
     ow = exchange(three, odd_w)
-    m2, product, factor, vt = call(
+    m2, product, factor, gram, reach = call(
         second_kernel,
         [
             ((3, 3 * atoms, w_rows), BF16),
             ((2, 3 * atoms // 2, 2 * width), F32),
             ((2, atoms, width), F32),
-            ((width, 3 * atoms), BF16),
+            ((2, width, width), F32),
+            ((2, width, 6 * w_rows), BF16),
         ],
         m1, near, ht, vectors, labels, masses, rim, ez, oz,
         scratch=[
             onehot_scr,
             pltpu.VMEM((3, 3 * atoms, w_base), BF16),
             pltpu.VMEM((3, w_base, 2 * width), BF16),
+            pltpu.VMEM((width, 3 * atoms), F32),
         ],
         cost=cost,
     )
-    image, mine, other = call(
-        apply_kernel,
-        [((2, 3 * atoms, width), F32), ((width, width), F32), ((width, width), F32)],
-        m1, m2, product, factor, vt, ew, ow,
-        scratch=[pltpu.VMEM((3, w_rows, 2 * width), BF16)],
+    mine, other, ext = call(
+        partial_kernel,
+        [((width, width), F32), ((width, width), F32), ((3 * w_rows, 2 * width), BF16)],
+        reach, gram, ew, ow,
+        cost=(24 * width * width * w_rows, 2**20),
+    )
+    (turned,) = call(
+        turn_kernel, [((2, 3 * atoms, width), F32)], m1, m2, product, factor, ext, rotation,
         cost=(2 * 18 * atoms * w_rows * 2 * width, 4 * 2**20),
-    )
-    (turned,) = call(
-        turn_kernel, [((2, 3 * atoms, width), F32)], image, rotation,
-        cost=(2 * 18 * atoms * width * width, 2**20),
     )
     total = mine + exchange(other, lambda p, q: (p ^ 1, q))
     bits = [(1 << k, 0) for k in range(1, n_wide.bit_length() - 1)]
@@ -372,22 +421,37 @@
     for k in range(0, len(bits), 2):
         steps = list(bits[k : k + 2])
         if len(steps) == 2:
-            steps.insert(0, (steps[0][0] ^ steps[1][0], steps[0][1] ^ steps[1][1]))
+            steps.append((steps[0][0] ^ steps[1][0], steps[0][1] ^ steps[1][1]))
         parts = [exchange(total, lambda p, q, s=s: (p ^ s[0], q ^ s[1])) for s in steps]
         for part in parts:
             total = total + part
+        if k == 0:
+            total, turned = lax.optimization_barrier((total, turned))
     other = exchange(total, lambda p, q: (p ^ 1, q))
     count = 3.0 * atoms * n_wide * n_narrow
-
-    def final(*refs):
-        final_kernel(*refs, count=count)
-
-    gram, rotated = call(
-        final,
-        [((2, width, width), F32), ((2, 3, atoms, width), BF16)],
-        total, other, turned, vectors, rotation,
-    )
-    return gram, rotated
+    outs = [
+        jax.ShapeDtypeStruct((2, width, width), F32),
+        jax.ShapeDtypeStruct((2, 3, atoms, width), BF16),
+    ]
+    hbm = pl.BlockSpec(memory_space=pltpu.HBM)
+
+    def finish(total, held=()):
+        return pl.pallas_call(
+            functools.partial(finish_kernel, count=count, own=not held),
+            out_shape=outs,
+            in_specs=[VMEM] * 4 + [hbm] * len(held),
+            out_specs=[hbm] * 2,
+            scratch_shapes=[
+                pltpu.VMEM((width, width), F32),
+                pltpu.VMEM((3, atoms, width), BF16),
+                pltpu.SemaphoreType.DMA((2,)),
+            ],
+            input_output_aliases={4: 0, 5: 1} if held else {},
+            compiler_params=pltpu.CompilerParams(vmem_limit_bytes=24 * 2**20),
+            cost_estimate=pl.CostEstimate(flops=10**6, bytes_accessed=10**6, transcendentals=0),
+        )(total, turned, vectors, rotation, *held)
+
+    return tuple(finish(other, finish(total)))
 
 
 def solution(mesh):

time: 35.6 us -> 33.7 us (0.947)
  waiting for transfers between devices: 13.4 us -> 9.41 us
  Pallas kernels: 6.32 us -> 8.16 us
    ppermute x12, waiting for transfers between devices: 13.4 us -> 9.41 us  [swap(): return lax.ppermute(array, AXES, pairs)]
    pallas_call x0 -> x2, Pallas kernels: none -> 2.14 us  [finish(): pl.pallas_call(functools.partial(finish_kernel, count=count, own=not held...]
    pallas_call x6 -> x5, Pallas kernels: 6.32 us -> 6.02 us  [call(): pl.pallas_call(kernel, out_shape=shapes, in_specs=[space] * len(args), ou...]
  transfers between devices with their start and end apart: 12 -> 12, of which waited for: 10 -> 9; matrix products, arithmetic and copies ran while one was open for 0% -> 0% of each run, Pallas kernels for 8% -> 16%
where the time goes in v3:
time: 33.7 us; the launch traced here: 33.6 us
  starting transfers between devices  15.2 us (45%)
  waiting for transfers between devices  9.41 us (28%)
  Pallas kernels  8.16 us (24%)
  between operations  0.71 us (2%)
    ppermute x12, starting transfers between devices, swap(): return lax.ppermute(array, AXES, pairs)  15.2 us
    ppermute x12, waiting for transfers between devices, swap(): return lax.ppermute(array, AXES, pairs)  9.41 us
    pallas_call x5, Pallas kernels, call(): pl.pallas_call(kernel, out_shape=shapes, in_specs=[space] * len(args), ou...  6.02 us
    pallas_call x2, Pallas kernels, finish(): pl.pallas_call(functools.partial(finish_kernel, count=count, own=not held...  2.14 us
  transfers between devices with their start and end apart: 12, of which 9 were waited for; matrix products, arithmetic and copies ran while one was open for 0% of the time, Pallas kernels for 16%

profile of v3, /device:TPU:0, one launch (start us, length us, event | category | flops | bytes accessed | tf_op | source)
XLA Modules:
  0.0 33.6 jit_solution(586509586858128744)
XLA Ops:
  0.6 1.2 %shard_map.86 = (bf16[4,32,128]{2,1,0:T(8,128)(2,1)S(1)}, bf16[3,128,128]{2,1,0:T(8,128)(2,1)S(1)}, s32[1,128]{1,0:T(1,128)S(1)}, f32[2,16]{1,0:T(2,128)S(1)}, s...) custom-call(bf16[3,128,128]{2,1,0:T(8,128)(2,1)} %vectors_hbm.1, ...), custom_call_target="tpu_custom_call" | custom-call | flops 1000 | bytes 1000 | tf_op jit(solution)/shard_map/pallas_call | solution.py:325
  1.8 0.6 %collective-permute-start.1 = (bf16[4,32,128]{2,1,0:T(8,128)(2,1)S(1)}, bf16[4,32,128]{2,1,0:T(8,128)(2,1)S(1)}, u32[]{:S(2)}, u32[]{:S(2)}) collective-permute-start(bf16[4,32,128]{2,1,0:T(8,128)(2,1)S(1)} %get-tuple-element.27.rim_ref), channel_id=1, source_target_pairs={{0,4},{1,2},{2,1},{3,7},{4,0},{5,6},{6,5},{7,3},{8,12},{9,10},{10,... | collective-permute-start | bytes 98312 | tf_op jit(solution)/shard_map/ppermute | solution.py:314
  2.4 4.1 %collective-permute-start = (bf16[4,32,128]{2,1,0:T(8,128)(2,1)S(1)}, bf16[4,32,128]{2,1,0:T(8,128)(2,1)S(1)}, u32[]{:S(2)}, u32[]{:S(2)}) collective-permute-start(bf16[4,32,128]{2,1,0:T(8,128)(2,1)S(1)} %get-tuple-element.27.rim_ref), channel_id=1, source_target_pairs={{0,1},{1,0},{2,3},{3,2},{4,5},{5,4},{6,7},{7,6},{8,9},{9,8},{10,11... | collective-permute-start | bytes 98312 | tf_op jit(solution)/shard_map/ppermute | solution.py:314
  6.5 1.1 %shard_map.87 = (bf16[3,384,512]{2,1,0:T(8,128)(2,1)S(1)}, s32[64,128]{1,0:T(8,128)S(1)}, bf16[9,128,128]{2,1,0:T(8,128)(2,1)S(1)}) custom-call(s32[60,128]{1,0:T(8,128)S(1)} %get-tuple-element.28.refs_0_, bf16[3,3,61,128]{3,2,1,0:T(8,128)(2,1)S(1)} %get-tuple-element.29.refs_1_), custom_call_target="tpu_custom_call" | custom-call | flops 603979776 | bytes 4194304 | tf_op jit(solution)/shard_map/pallas_call | solution.py:325
  7.7 0.0 collective-permute-done.1.oz_ref
  7.7 0.7 %collective-permute-done.ez_ref = bf16[4,32,128]{2,1,0:T(8,128)(2,1)S(1)} collective-permute-done((bf16[4,32,128]{2,1,0:T(8,128)(2,1)S(1)}, bf16[4,32,128]{2,1,0:T(8,128)(2,1)S(1)}, u32[]{:S(2)}, u32[]{:S(2)}) %collective-permute-start) | collective-permute-done | bytes 32800 | tf_op jit(solution)/shard_map/ppermute | solution.py:314
  8.4 2.1 %collective-permute-start.3 = (bf16[3,4,32,128]{3,2,1,0:T(8,128)(2,1)S(1)}, bf16[3,4,32,128]{3,2,1,0:T(8,128)(2,1)S(1)}, u32[]{:S(2)}, u32[]{:S(2)}) collective-permute-start(bf16[3,4,32,128]{3,2,1,0:T(8,128)(2,1)S(1)} %pad_maximum_fusion), channel_id=1, source_target_pairs={{0,1},{1,0},{2,3},{3,2},{4,8},{5,9},{6,10},{7,11},{8,4},{9,5},{10,... | collective-permute-start | bytes 294920 | tf_op jit(solution)/shard_map/ppermute | solution.py:314
  10.5 0.0 collective-permute-start.2
  10.5 2.4 %shard_map.88 = (bf16[3,384,256]{2,1,0:T(8,128)(2,1)S(1)}, f32[2,192,256]{2,1,0:T(8,128)S(1)}, f32[2,128,128]{2,1,0:T(8,128)S(1)}, f32[2,128,128]{2,1,0:T(8,128)S(1)}, bf16[2,128,1536]{2,1,0:T(8,128)(2,1)S(1)}) custom-call(bf16[3,384,512]{2,1,0:T(8,128)(2,1)S(1)} %get-tuple-element.31.m1_ref, s32[64,128]{1,0:T(8,128)S(1)} %get-tuple-element.32.near_ref, ...), custom_call_target="tpu_custom_call" | custom-call | flops 603979776 | bytes 4194304 | tf_op jit(solution)/shard_map/pallas_call | solution.py:325
  12.9 0.2 collective-permute-done.3.ow_ref
  13.1 0.0 collective-permute-done.2.ew_ref
  13.1 0.6 %shard_map.89 = (f32[128,128]{1,0:T(8,128)S(1)}, f32[128,128]{1,0:T(8,128)S(1)}, bf16[768,256]{1,0:T(8,128)(2,1)S(1)}) custom-call(bf16[2,128,1536]{2,1,0:T(8,128)(2,1)S(1)} %get-tuple-element.39.reach_ref, f32[2,128,128]{2,1,0:T(8,128)S(1)} %get-tuple-element.40.gram_ref, bf16[3,4,32,128]{3,2,1,0:T(8,128)(2,1)S(1)} %collective-permute-done.2.ew_ref, ...), custom_call_target="tpu_custom_call" | custom-call | flops 100663296 | bytes 1048576 | tf_op jit(solution)/shard_map/pallas_call | solution.py:325
  13.7 0.4 %collective-permute-start.4 = (f32[128,128]{1,0:T(8,128)S(1)}, f32[128,128]{1,0:T(8,128)S(1)}, u32[]{:S(2)}, u32[]{:S(2)}) collective-permute-start(f32[128,128]{1,0:T(8,128)S(1)} %get-tuple-element.42), channel_id=1, source_target_pairs={{0,4},{1,5},{2,6},{3,7},{4,0},{5,1},{6,2},{7,3},{8,12},{9,13},{10,... | collective-permute-start | bytes 196616 | tf_op jit(solution)/shard_map/ppermute | solution.py:314
  14.1 0.9 %collective-permute-done.4 = f32[128,128]{1,0:T(8,128)S(1)} collective-permute-done((f32[128,128]{1,0:T(8,128)S(1)}, f32[128,128]{1,0:T(8,128)S(1)}, u32[]{:S(2)}, u32[]{:S(2)}) %collective-permute-start.4) | collective-permute-done | bytes 65568 | tf_op jit(solution)/shard_map/ppermute | solution.py:314
  15.0 2.1 %collective-permute-start.7 = (f32[128,128]{1,0:T(8,128)S(1)}, f32[128,128]{1,0:T(8,128)S(1)}, u32[]{:S(2)}, u32[]{:S(2)}) collective-permute-start(f32[128,128]{1,0:T(8,128)S(1)} %add.21), channel_id=1, source_target_pairs={{0,24},{1,25},{2,26},{3,27},{4,28},{5,29},{6,30},{7,31},{8,16},{9,... | collective-permute-start | bytes 196616 | tf_op jit(solution)/shard_map/ppermute | solution.py:314
  17.1 0.4 %collective-permute-start.6 = (f32[128,128]{1,0:T(8,128)S(1)}, f32[128,128]{1,0:T(8,128)S(1)}, u32[]{:S(2)}, u32[]{:S(2)}) collective-permute-start(f32[128,128]{1,0:T(8,128)S(1)} %add.21), channel_id=1, source_target_pairs={{0,16},{1,17},{2,18},{3,19},{4,20},{5,21},{6,22},{7,23},{8,24},{9,... | collective-permute-start | bytes 196616 | tf_op jit(solution)/shard_map/ppermute | solution.py:314
  17.5 1.1 %collective-permute-start.5 = (f32[128,128]{1,0:T(8,128)S(1)}, f32[128,128]{1,0:T(8,128)S(1)}, u32[]{:S(2)}, u32[]{:S(2)}) collective-permute-start(f32[128,128]{1,0:T(8,128)S(1)} %add.21), channel_id=1, source_target_pairs={{0,8},{1,9},{2,10},{3,11},{4,12},{5,13},{6,14},{7,15},{8,0},{9,1},... | collective-permute-start | bytes 196616 | tf_op jit(solution)/shard_map/ppermute | solution.py:314
  18.6 0.7 %shard_map.90.turned_ref = f32[2,384,128]{2,1,0:T(8,128)S(1)} custom-call(bf16[3,384,512]{2,1,0:T(8,128)(2,1)S(1)} %get-tuple-element.31.m1_ref, bf16[3,384,256]{2,1,0:T(8,128)(2,1)S(1)} %get-tuple-element.43.m2_ref, f32[2,192,256]{2,1,0:T(8,128)S(1)} %get-tuple-element.44.product_ref, f32[2,128,128]{2,1,0:T(8,128)S(1)} %get-tuple-element.45.factor_ref, ...), custom_call_target="tpu_custom_call" | custom-call | flops 301989888 | bytes 4194304 | tf_op jit(solution)/shard_map/pallas_call | solution.py:325
  19.3 1.1 %collective-permute-done.7 = f32[128,128]{1,0:T(8,128)S(1)} collective-permute-done((f32[128,128]{1,0:T(8,128)S(1)}, f32[128,128]{1,0:T(8,128)S(1)}, u32[]{:S(2)}, u32[]{:S(2)}) %collective-permute-start.7) | collective-permute-done | bytes 65568 | tf_op jit(solution)/shard_map/ppermute | solution.py:314
  20.4 1.3 %collective-permute-done.6 = f32[128,128]{1,0:T(8,128)S(1)} collective-permute-done((f32[128,128]{1,0:T(8,128)S(1)}, f32[128,128]{1,0:T(8,128)S(1)}, u32[]{:S(2)}, u32[]{:S(2)}) %collective-permute-start.6) | collective-permute-done | bytes 65568 | tf_op jit(solution)/shard_map/ppermute | solution.py:314
  21.7 0.4 %collective-permute-done.5 = f32[128,128]{1,0:T(8,128)S(1)} collective-permute-done((f32[128,128]{1,0:T(8,128)S(1)}, f32[128,128]{1,0:T(8,128)S(1)}, u32[]{:S(2)}, u32[]{:S(2)}) %collective-permute-start.5) | collective-permute-done | bytes 65568 | tf_op jit(solution)/shard_map/ppermute | solution.py:314
  22.1 2.7 %collective-permute-start.10 = (f32[128,128]{1,0:T(8,128)S(1)}, f32[128,128]{1,0:T(8,128)S(1)}, u32[]{:S(2)}, u32[]{:S(2)}) collective-permute-start(f32[128,128]{1,0:T(8,128)S(1)} %add_add_fusion.1), channel_id=1, source_target_pairs={{0,3},{1,2},{2,1},{3,0},{4,7},{5,6},{6,5},{7,4},{8,11},{9,10},{10,... | collective-permute-start | bytes 196616 | tf_op jit(solution)/shard_map/ppermute | solution.py:314
  24.8 0.8 %collective-permute-start.9 = (f32[128,128]{1,0:T(8,128)S(1)}, f32[128,128]{1,0:T(8,128)S(1)}, u32[]{:S(2)}, u32[]{:S(2)}) collective-permute-start(f32[128,128]{1,0:T(8,128)S(1)} %add_add_fusion.1), channel_id=1, source_target_pairs={{0,2},{1,3},{2,0},{3,1},{4,6},{5,7},{6,4},{7,5},{8,10},{9,11},{10,... | collective-permute-start | bytes 196616 | tf_op jit(solution)/shard_map/ppermute | solution.py:314
  25.7 0.9 %collective-permute-start.8 = (f32[128,128]{1,0:T(8,128)S(1)}, f32[128,128]{1,0:T(8,128)S(1)}, u32[]{:S(2)}, u32[]{:S(2)}) collective-permute-start(f32[128,128]{1,0:T(8,128)S(1)} %add_add_fusion.1), channel_id=1, source_target_pairs={{0,1},{1,0},{2,3},{3,2},{4,5},{5,4},{6,7},{7,6},{8,9},{9,8},{10,11... | collective-permute-start | bytes 196616 | tf_op jit(solution)/shard_map/ppermute | solution.py:314
  26.6 1.8 %collective-permute-done.10 = f32[128,128]{1,0:T(8,128)S(1)} collective-permute-done((f32[128,128]{1,0:T(8,128)S(1)}, f32[128,128]{1,0:T(8,128)S(1)}, u32[]{:S(2)}, u32[]{:S(2)}) %collective-permute-start.10) | collective-permute-done | bytes 65568 | tf_op jit(solution)/shard_map/ppermute | solution.py:314
  28.3 2.8 %collective-permute-done.9 = f32[128,128]{1,0:T(8,128)S(1)} collective-permute-done((f32[128,128]{1,0:T(8,128)S(1)}, f32[128,128]{1,0:T(8,128)S(1)}, u32[]{:S(2)}, u32[]{:S(2)}) %collective-permute-start.9) | collective-permute-done | bytes 65568 | tf_op jit(solution)/shard_map/ppermute | solution.py:314
  31.1 0.0 collective-permute-done.8
  31.2 0.1 collective-permute-start.11
  31.3 1.1 %shard_map.91 = (f32[2,128,128]{2,1,0:T(8,128)}, bf16[2,3,128,128]{3,2,1,0:T(8,128)(2,1)}) custom-call(f32[128,128]{1,0:T(8,128)S(1)} %add_add_fusion.total_ref, f32[2,384,128]{2,1,0:T(8,128)S(1)} %shard_map.90.turned_ref, bf16[3,128,128]{2,1,0:T(8,128)(2,1)S(1)} %get-tuple-element.34.vectors_ref, f32[2,128,128]{2,1,0:T(8,128)S(1)} %get-tuple-element.47.rotation_ref), custom_call_target="tpu_custom_call" | custom-call | flops 1000000 | bytes 1000000 | tf_op jit(solution)/shard_map/pallas_call | solution.py:439
  32.4 0.2 collective-permute-done.11.total_ref
  32.5 1.1 %shard_map.92 = (f32[2,128,128]{2,1,0:T(8,128)}, bf16[2,3,128,128]{3,2,1,0:T(8,128)(2,1)}) custom-call(f32[128,128]{1,0:T(8,128)S(1)} %collective-permute-done.11.total_ref, f32[2,384,128]{2,1,0:T(8,128)S(1)} %shard_map.90.turned_ref, bf16[3,128,128]{2,1,0:T(8,128)(2,1)S(1)} %get-tuple-element.34.vectors_ref, ...), custom_call_target="tpu_custom_call", output_to_operand_aliasing={{0}: (4, {}), {1}: (5, {})} | custom-call | flops 1000000 | bytes 1000000 | tf_op jit(solution)/shard_map/pallas_call | solution.py:439
  (4 shorter events, 0.1 us)
Async XLA Ops:
  1.8 5.8 %collective-permute-start.1 = (bf16[4,32,128]{2,1,0:T(8,128)(2,1)S(1)}, bf16[4,32,128]{2,1,0:T(8,128)(2,1)S(1)}, u32[]{:S(2)}, u32[]{:S(2)}) collective-permute-start(bf16[4,32,128]{2,1,0:T(8,128)(2,1)S(1)} %get-tuple-element.27.rim_ref), channel_id=1, source_target_pairs={{0,4},{1,2},{2,1},{3,7},{4,0},{5,6},{6,5},{7,3},{8,12},{9,10},{10,... | collective-permute-start | bytes 98312 | tf_op jit(solution)/shard_map/ppermute | solution.py:314
  2.4 6.0 %collective-permute-start = (bf16[4,32,128]{2,1,0:T(8,128)(2,1)S(1)}, bf16[4,32,128]{2,1,0:T(8,128)(2,1)S(1)}, u32[]{:S(2)}, u32[]{:S(2)}) collective-permute-start(bf16[4,32,128]{2,1,0:T(8,128)(2,1)S(1)} %get-tuple-element.27.rim_ref), channel_id=1, source_target_pairs={{0,1},{1,0},{2,3},{3,2},{4,5},{5,4},{6,7},{7,6},{8,9},{9,8},{10,11... | collective-permute-start | bytes 98312 | tf_op jit(solution)/shard_map/ppermute | solution.py:314
  8.4 4.7 %collective-permute-start.3 = (bf16[3,4,32,128]{3,2,1,0:T(8,128)(2,1)S(1)}, bf16[3,4,32,128]{3,2,1,0:T(8,128)(2,1)S(1)}, u32[]{:S(2)}, u32[]{:S(2)}) collective-permute-start(bf16[3,4,32,128]{3,2,1,0:T(8,128)(2,1)S(1)} %pad_maximum_fusion), channel_id=1, source_target_pairs={{0,1},{1,0},{2,3},{3,2},{4,8},{5,9},{6,10},{7,11},{8,4},{9,5},{10,... | collective-permute-start | bytes 294920 | tf_op jit(solution)/shard_map/ppermute | solution.py:314
  10.5 2.6 %collective-permute-start.2 = (bf16[3,4,32,128]{3,2,1,0:T(8,128)(2,1)S(1)}, bf16[3,4,32,128]{3,2,1,0:T(8,128)(2,1)S(1)}, u32[]{:S(2)}, u32[]{:S(2)}) collective-permute-start(bf16[3,4,32,128]{3,2,1,0:T(8,128)(2,1)S(1)} %pad_maximum_fusion), channel_id=1, source_target_pairs={{0,4},{1,5},{2,6},{3,7},{4,0},{5,1},{6,2},{7,3},{8,12},{9,13},{10,... | collective-permute-start | bytes 294920 | tf_op jit(solution)/shard_map/ppermute | solution.py:314
  13.7 1.3 %collective-permute-start.4 = (f32[128,128]{1,0:T(8,128)S(1)}, f32[128,128]{1,0:T(8,128)S(1)}, u32[]{:S(2)}, u32[]{:S(2)}) collective-permute-start(f32[128,128]{1,0:T(8,128)S(1)} %get-tuple-element.42), channel_id=1, source_target_pairs={{0,4},{1,5},{2,6},{3,7},{4,0},{5,1},{6,2},{7,3},{8,12},{9,13},{10,... | collective-permute-start | bytes 196616 | tf_op jit(solution)/shard_map/ppermute | solution.py:314
  15.0 5.4 %collective-permute-start.7 = (f32[128,128]{1,0:T(8,128)S(1)}, f32[128,128]{1,0:T(8,128)S(1)}, u32[]{:S(2)}, u32[]{:S(2)}) collective-permute-start(f32[128,128]{1,0:T(8,128)S(1)} %add.21), channel_id=1, source_target_pairs={{0,24},{1,25},{2,26},{3,27},{4,28},{5,29},{6,30},{7,31},{8,16},{9,... | collective-permute-start | bytes 196616 | tf_op jit(solution)/shard_map/ppermute | solution.py:314
  17.1 4.6 %collective-permute-start.6 = (f32[128,128]{1,0:T(8,128)S(1)}, f32[128,128]{1,0:T(8,128)S(1)}, u32[]{:S(2)}, u32[]{:S(2)}) collective-permute-start(f32[128,128]{1,0:T(8,128)S(1)} %add.21), channel_id=1, source_target_pairs={{0,16},{1,17},{2,18},{3,19},{4,20},{5,21},{6,22},{7,23},{8,24},{9,... | collective-permute-start | bytes 196616 | tf_op jit(solution)/shard_map/ppermute | solution.py:314
  17.5 4.6 %collective-permute-start.5 = (f32[128,128]{1,0:T(8,128)S(1)}, f32[128,128]{1,0:T(8,128)S(1)}, u32[]{:S(2)}, u32[]{:S(2)}) collective-permute-start(f32[128,128]{1,0:T(8,128)S(1)} %add.21), channel_id=1, source_target_pairs={{0,8},{1,9},{2,10},{3,11},{4,12},{5,13},{6,14},{7,15},{8,0},{9,1},... | collective-permute-start | bytes 196616 | tf_op jit(solution)/shard_map/ppermute | solution.py:314
  22.1 6.2 %collective-permute-start.10 = (f32[128,128]{1,0:T(8,128)S(1)}, f32[128,128]{1,0:T(8,128)S(1)}, u32[]{:S(2)}, u32[]{:S(2)}) collective-permute-start(f32[128,128]{1,0:T(8,128)S(1)} %add_add_fusion.1), channel_id=1, source_target_pairs={{0,3},{1,2},{2,1},{3,0},{4,7},{5,6},{6,5},{7,4},{8,11},{9,10},{10,... | collective-permute-start | bytes 196616 | tf_op jit(solution)/shard_map/ppermute | solution.py:314
  24.8 6.3 %collective-permute-start.9 = (f32[128,128]{1,0:T(8,128)S(1)}, f32[128,128]{1,0:T(8,128)S(1)}, u32[]{:S(2)}, u32[]{:S(2)}) collective-permute-start(f32[128,128]{1,0:T(8,128)S(1)} %add_add_fusion.1), channel_id=1, source_target_pairs={{0,2},{1,3},{2,0},{3,1},{4,6},{5,7},{6,4},{7,5},{8,10},{9,11},{10,... | collective-permute-start | bytes 196616 | tf_op jit(solution)/shard_map/ppermute | solution.py:314
  25.7 5.5 %collective-permute-start.8 = (f32[128,128]{1,0:T(8,128)S(1)}, f32[128,128]{1,0:T(8,128)S(1)}, u32[]{:S(2)}, u32[]{:S(2)}) collective-permute-start(f32[128,128]{1,0:T(8,128)S(1)} %add_add_fusion.1), channel_id=1, source_target_pairs={{0,1},{1,0},{2,3},{3,2},{4,5},{5,4},{6,7},{7,6},{8,9},{9,8},{10,11... | collective-permute-start | bytes 196616 | tf_op jit(solution)/shard_map/ppermute | solution.py:314
  31.2 1.3 %collective-permute-start.11 = (f32[128,128]{1,0:T(8,128)S(1)}, f32[128,128]{1,0:T(8,128)S(1)}, u32[]{:S(2)}, u32[]{:S(2)}) collective-permute-start(f32[128,128]{1,0:T(8,128)S(1)} %add_add_fusion.total_ref), channel_id=1, source_target_pairs={{0,4},{1,5},{2,6},{3,7},{4,0},{5,1},{6,2},{7,3},{8,12},{9,13},{10,... | collective-permute-start | bytes 196616 | tf_op jit(solution)/shard_map/ppermute | solution.py:314
